TPU v7x, 32 devices: a whole 2x2x4 slice. The times are simulated.
32 devices in a mesh: dp: 8 (over z, x), seq: 4 (over y, core).
Axes of the slice: x: 2, y: 2, z: 4, core: 2. Of those that a mesh axis runs over, the one named last changes fastest.
Arguments:
- tokens: bfloat16 [96, 512, 768], P('dp', 'seq'), may hold values from -6 to 6
- lengths: int32 [96], P('dp'), may hold values from 20 to 512, as said below
- cotangent: bfloat16 [96, 512, 768], P('dp', 'seq'), may hold values from -6 to 6
- w_query: bfloat16 [768, 768], replicated, may hold values from -0.21875 to 0.21875
- w_key: bfloat16 [768, 768], replicated, may hold values from -0.21875 to 0.21875
- w_value: bfloat16 [768, 768], replicated, may hold values from -0.21875 to 0.21875
- w_out: bfloat16 [768, 768], replicated, may hold values from -0.875 to 0.875
- w_inner: bfloat16 [768, 3072], replicated, may hold values from -0.21875 to 0.21875
- w_outer: bfloat16 [3072, 768], replicated, may hold values from -0.109375 to 0.109375
- down_one: bfloat16 [768, 64], replicated, may hold values from -0.21875 to 0.21875
- up_one: bfloat16 [64, 768], replicated, may hold values from -0.75 to 0.75
- down_two: bfloat16 [768, 64], replicated, may hold values from -0.21875 to 0.21875
- up_two: bfloat16 [64, 768], replicated, may hold values from -0.75 to 0.75
- gain_one: float32 [768], replicated, may hold values from 0.5 to 1.5
- bias_one: float32 [768], replicated, may hold values from -3 to 3
- gain_two: float32 [768], replicated, may hold values from 0.5 to 1.5
- bias_two: float32 [768], replicated, may hold values from -3 to 3
Outputs:
- output: bfloat16 [96, 512, 768], P('dp', 'seq')
- input_grad: float32 [96, 512, 768], P('dp', 'seq')
- grad_down_one: float32 [768, 64], replicated
- grad_up_one: float32 [64, 768], replicated
- grad_down_two: float32 [768, 64], replicated
- grad_up_two: float32 [64, 768], replicated
- grad_gain_one: float32 [768], replicated
- grad_bias_one: float32 [768], replicated
- grad_gain_two: float32 [768], replicated
- grad_bias_two: float32 [768], replicated
Inputs may be any that keep to these rules, and one draw needn't show every extreme that they name: `lengths`: among the 12 sequences of each index of dp, one has exactly 512 tokens and another exactly 20.
All inputs are finite; a program needn't handle non-finite values.
Results may differ from a plain program's by a relative error of at most 0.015.
Values may be sent and summed in bfloat16 or wider, within the bound.
A program may use at most 320 MiB of HBM per device.

v0:
```python
import jax
import jax.numpy as jnp
from jax import lax
from jax.sharding import PartitionSpec as P

HEADS = 12


EPS = 1e-06


def matmul(left, right):
    return jnp.dot(left, right, preferred_element_type=jnp.float32)


def matmul_rt(left, right):
    return lax.dot_general(
        left, right, (((1,), (1,)), ((), ())), preferred_element_type=jnp.float32
    )


def matmul_lt(left, right):
    return lax.dot_general(
        left, right, (((0,), (0,)), ((), ())), preferred_element_type=jnp.float32
    )


def gelu_slope(value):
    return (
        0.5 * (1.0 + lax.erf(value * 0.7071067811865476))
        + value * jnp.exp(-0.5 * value * value) * 0.3989422804014327
    )


def norm_forward(hidden, gain, bias):
    mean = jnp.mean(hidden, axis=-1, keepdims=True)
    centred = hidden - mean
    inverse = lax.rsqrt(jnp.mean(centred * centred, axis=-1, keepdims=True) + EPS)
    normed = centred * inverse
    return (normed * gain + bias, normed, inverse)


def norm_backward(grad, normed, inverse, gain):
    scaled = grad * gain
    inner = (
        scaled
        - jnp.mean(scaled, axis=-1, keepdims=True)
        - normed * jnp.mean(scaled * normed, axis=-1, keepdims=True)
    )
    return (inner * inverse, jnp.sum(grad * normed, axis=0), jnp.sum(grad, axis=0))


def split_pair(values):
    upper = values.astype(jnp.bfloat16)
    lower = (values - upper.astype(jnp.float32)).astype(jnp.bfloat16)
    return (upper, lower)


def attend_forward(block):
    query, key, value, valid = block
    scale = query.shape[-1] ** (-0.5)
    scores = jnp.einsum("gqhd,gnkhd->ghqnk", query, key, preferred_element_type=jnp.float32) * scale
    mask = valid[:, None, None, :, :]
    masked = jnp.where(mask, scores, -1e30)
    top = jnp.max(masked, axis=4, keepdims=True)
    expo = jnp.where(mask, jnp.exp(masked - top), 0.0)
    total = jnp.sum(expo, axis=4, keepdims=True)
    peak = jnp.max(top, axis=3, keepdims=True)
    weight = jnp.exp(top - peak)
    denom = jnp.sum(total * weight, axis=3)
    part = jnp.einsum(
        "ghqnk,gnkhd->ghqnd", expo.astype(jnp.bfloat16), value, preferred_element_type=jnp.float32
    )
    attn = jnp.sum(part * weight, axis=3) / denom
    lse = peak[:, :, :, :, 0] + jnp.log(denom)
    return (attn.transpose(0, 2, 1, 3), top, lse)


def attend_backward(block):
    query, key, value, valid, top, lse, grad_ctx, attn = block
    scale = query.shape[-1] ** (-0.5)
    scores = jnp.einsum("gqhd,gnkhd->ghqnk", query, key, preferred_element_type=jnp.float32) * scale
    mask = valid[:, None, None, :, :]
    expo = jnp.where(mask, jnp.exp(jnp.where(mask, scores, -1e30) - top), 0.0)
    prob = jnp.where(mask, jnp.exp(scores - lse[..., None]), 0.0)
    grad_prob = jnp.einsum("gqhd,gnkhd->ghqnk", grad_ctx, value, preferred_element_type=jnp.float32)
    grad_wide = grad_ctx.astype(jnp.float32)
    delta = jnp.sum(grad_wide * attn, axis=3).transpose(0, 2, 1)[..., None, None]
    grad_scores = (prob * (grad_prob - delta)).astype(jnp.bfloat16)
    grad_query = (
        jnp.einsum("ghqnk,gnkhd->gqhd", grad_scores, key, preferred_element_type=jnp.float32)
        * scale
    )
    grad_key = (
        jnp.einsum("ghqnk,gqhd->gnkhd", grad_scores, query, preferred_element_type=jnp.float32)
        * scale
    )
    factor = jnp.exp(top - lse[..., None]).transpose(0, 3, 2, 1, 4)
    weighted = grad_wide[:, None, :, :, :] * factor
    upper, lower = split_pair(weighted)
    expo_low = expo.astype(jnp.bfloat16)
    grad_value = jnp.einsum(
        "ghqnk,gnqhd->gnkhd", expo_low, upper, preferred_element_type=jnp.float32
    )
    grad_value = grad_value + jnp.einsum(
        "ghqnk,gnqhd->gnkhd", expo_low, lower, preferred_element_type=jnp.float32
    )
    return (grad_query, grad_key, grad_value)


def per_device(
    tokens,
    lengths,
    cotangent,
    w_query,
    w_key,
    w_value,
    w_out,
    w_inner,
    w_outer,
    down_one,
    up_one,
    down_two,
    up_two,
    gain_one,
    bias_one,
    gain_two,
    bias_two,
):
    batch, rows, width = tokens.shape
    parts = lax.axis_size("seq")
    heads = HEADS
    head = width // heads
    count = batch * rows
    whole = parts * rows
    span = max(1, min(batch, 512 // rows))
    blocks = batch // span
    flat = tokens.reshape(count, width)
    query = matmul(flat, w_query).astype(jnp.bfloat16)
    key_own = matmul(flat, w_key).astype(jnp.bfloat16).reshape(batch, rows, width)
    value_own = matmul(flat, w_value).astype(jnp.bfloat16).reshape(batch, rows, width)
    key_all, value_all = (
        lax.all_gather(key_own, "seq", axis=1, tiled=True),
        lax.all_gather(value_own, "seq", axis=1, tiled=True),
    )
    valid = jnp.arange(whole).reshape(1, parts, rows) < lengths.reshape(batch, 1, 1)
    query_blocks = query.reshape(blocks, span, rows, heads, head)
    key_blocks = key_all.reshape(blocks, span, parts, rows, heads, head)
    value_blocks = value_all.reshape(blocks, span, parts, rows, heads, head)
    valid_blocks = valid.reshape(blocks, span, parts, rows)
    attn, top, lse = lax.map(attend_forward, (query_blocks, key_blocks, value_blocks, valid_blocks))
    ctx = attn.reshape(count, width).astype(jnp.bfloat16)
    out_proj = matmul(ctx, w_out)
    out_low = out_proj.astype(jnp.bfloat16)
    zed_one = matmul(out_low, down_one)
    gelu_one = jax.nn.gelu(zed_one, approximate=False).astype(jnp.bfloat16)
    branch_one = matmul(gelu_one, up_one)
    hidden_one = flat.astype(jnp.float32) + out_proj + branch_one
    normed_one, unit_one, inverse_one = norm_forward(hidden_one, gain_one, bias_one)
    normed_low = normed_one.astype(jnp.bfloat16)
    inner = matmul(normed_low, w_inner)
    hidden_low = jax.nn.gelu(inner, approximate=False).astype(jnp.bfloat16)
    ffn_out = matmul(hidden_low, w_outer)
    ffn_low = ffn_out.astype(jnp.bfloat16)
    zed_two = matmul(ffn_low, down_two)
    gelu_two = jax.nn.gelu(zed_two, approximate=False).astype(jnp.bfloat16)
    branch_two = matmul(gelu_two, up_two)
    hidden_two = normed_one + ffn_out + branch_two
    result, unit_two, inverse_two = norm_forward(hidden_two, gain_two, bias_two)
    output = result.astype(jnp.bfloat16).reshape(batch, rows, width)
    grad_out = cotangent.reshape(count, width).astype(jnp.float32)
    grad_two, grad_gain_two, grad_bias_two = norm_backward(
        grad_out, unit_two, inverse_two, gain_two
    )
    grad_branch_two = grad_two.astype(jnp.bfloat16)
    grad_up_two = matmul_lt(gelu_two, grad_branch_two)
    grad_zed_two = (matmul_rt(grad_branch_two, up_two) * gelu_slope(zed_two)).astype(jnp.bfloat16)
    grad_down_two = matmul_lt(ffn_low, grad_zed_two)
    grad_ffn = (grad_two + matmul_rt(grad_zed_two, down_two)).astype(jnp.bfloat16)
    grad_inner = (matmul_rt(grad_ffn, w_outer) * gelu_slope(inner)).astype(jnp.bfloat16)
    grad_normed = grad_two + matmul_rt(grad_inner, w_inner)
    grad_one, grad_gain_one, grad_bias_one = norm_backward(
        grad_normed, unit_one, inverse_one, gain_one
    )
    grad_branch_one = grad_one.astype(jnp.bfloat16)
    grad_up_one = matmul_lt(gelu_one, grad_branch_one)
    grad_zed_one = (matmul_rt(grad_branch_one, up_one) * gelu_slope(zed_one)).astype(jnp.bfloat16)
    grad_down_one = matmul_lt(out_low, grad_zed_one)
    grad_proj = (grad_one + matmul_rt(grad_zed_one, down_one)).astype(jnp.bfloat16)
    grad_ctx = matmul_rt(grad_proj, w_out).astype(jnp.bfloat16)
    grad_ctx_blocks = grad_ctx.reshape(blocks, span, rows, heads, head)
    grad_query, grad_key, grad_value = lax.map(
        attend_backward,
        (query_blocks, key_blocks, value_blocks, valid_blocks, top, lse, grad_ctx_blocks, attn),
    )
    key_terms = grad_key.reshape(batch, whole, width)
    value_terms = grad_value.reshape(batch, whole, width)
    key_sum, value_sum = (
        lax.psum_scatter(
            key_terms.astype(jnp.bfloat16), "seq", scatter_dimension=1, tiled=True
        ).astype(jnp.float32),
        lax.psum_scatter(
            value_terms.astype(jnp.bfloat16), "seq", scatter_dimension=1, tiled=True
        ).astype(jnp.float32),
    )
    grad_query = grad_query.reshape(count, width).astype(jnp.bfloat16)
    grad_key_low = key_sum.reshape(count, width).astype(jnp.bfloat16)
    grad_value_low = value_sum.reshape(count, width).astype(jnp.bfloat16)
    grad_input = (
        grad_one
        + matmul_rt(grad_query, w_query)
        + matmul_rt(grad_key_low, w_key)
        + matmul_rt(grad_value_low, w_value)
    )
    sums = lax.psum(
        (
            grad_down_one,
            grad_up_one,
            grad_down_two,
            grad_up_two,
            grad_gain_one,
            grad_bias_one,
            grad_gain_two,
            grad_bias_two,
        ),
        ("dp", "seq"),
    )
    return (
        output,
        grad_input.reshape(batch, rows, width),
        sums[0],
        sums[1],
        sums[2],
        sums[3],
        sums[4],
        sums[5],
        sums[6],
        sums[7],
    )


def solution(mesh):
    placed = (
        P("dp", "seq", None),
        P("dp"),
        P("dp", "seq", None),
        P(),
        P(),
        P(),
        P(),
        P(),
        P(),
        P(),
        P(),
        P(),
        P(),
        P(),
        P(),
        P(),
        P(),
    )
    return jax.shard_map(
        per_device,
        mesh=mesh,
        in_specs=placed,
        out_specs=(
            P("dp", "seq", None),
            P("dp", "seq", None),
            P(),
            P(),
            P(),
            P(),
            P(),
            P(),
            P(),
            P(),
        ),
        check_vma=False,
    )
```

profile of v0, /device:TPU:1, one launch (start us, length us, event | category | flops | bytes accessed | tf_op | source)
XLA Modules:
  0.0 862.8 jit_solution(5557883260030518720)
XLA Ops:
  38.4 43.6 %all-gather.5.cloned.1.call-done = bf16[12,512,768]{1,2,0:T(8,128)(2,1)} async-done(((bf16[12,128,768]{1,2,0:T(8,128)(2,1)}), bf16[12,512,768]{1,2,0:T(8,128)(2,1)}) %all-gather.5.cloned.1.call-update) | async-done | bytes 9437200 | tf_op jit(solution)/shard_map/all_gather | solution.py:143
  82.0 14.3 %reshape.218 = bf16[3,4,4,128,12,64]{3,2,5,4,1,0:T(4,128)(2,1)} reshape(bf16[12,512,768]{1,2,0:T(8,128)(2,1)} %all-gather.5.cloned.1.call-done) | data formatting | bytes 18874368 | tf_op jit(solution)/shard_map/reshape | solution.py:148
  96.3 10.5 %copy.94 = bf16[3,4,4,128,12,64]{3,5,2,4,1,0:T(8,128)(2,1)} copy(bf16[3,4,4,128,12,64]{3,2,5,4,1,0:T(4,128)(2,1)} %reshape.218) | data formatting | bytes 18874368 | tf_op jit(solution)/shard_map/while | solution.py:151
  106.8 42.8 %all-gather.3.cloned.1.call-done = bf16[12,512,768]{1,2,0:T(8,128)(2,1)} async-done(((bf16[12,128,768]{1,2,0:T(8,128)(2,1)}), bf16[12,512,768]{1,2,0:T(8,128)(2,1)}) %all-gather.3.cloned.1.call-update) | async-done | bytes 9437200 | tf_op jit(solution)/shard_map/all_gather | solution.py:144
  149.6 13.9 %reshape.212 = bf16[3,4,4,128,12,64]{3,2,5,4,1,0:T(4,128)(2,1)} reshape(bf16[12,512,768]{1,2,0:T(8,128)(2,1)} %all-gather.3.cloned.1.call-done) | data formatting | bytes 18874368 | tf_op jit(solution)/shard_map/reshape | solution.py:149
  163.5 10.3 %copy.92 = bf16[3,4,4,128,12,64]{3,5,2,4,1,0:T(8,128)(2,1)} copy(bf16[3,4,4,128,12,64]{3,2,5,4,1,0:T(4,128)(2,1)} %reshape.212) | data formatting | bytes 18874368 | tf_op jit(solution)/shard_map/while | solution.py:151
  173.8 68.2 %while.30 = (s32[]{:T(128)}, f32[3,4,128,12,64]{2,4,3,1,0:T(8,128)}, f32[3,4,12,128,4,1]{3,4,2,1,5,0:T(4,128)}, f32[3,4,12,128,1]{3,2,1,4,0:T(8,128)}, bf16[3,4,...) while((s32[]{:T(128)}, ...), condition=%wide.region_6.7_spmd.clone, body=%wide.region_0.6_spmd.sunk.clone | while | flops 852510720 | bytes 50842764 | solution.py:151
  184.5 7.1 fusion.262
  207.1 7.1 fusion.262
  229.8 7.1 fusion.262
  264.2 11.0 %fusion.96 = f32[1536,3072]{1,0:T(8,128)} fusion(bf16[768,3072]{1,0:T(8,128)(2,1)S(1)} %bitcast.307, f32[1536,768]{1,0:T(8,128)S(1)} %get-tuple-element.271, f32[768]{0:T(1024)S(1)} %copy-done.45, f32[768]{0:T(1024)S(1)} %copy-done.41, f32[1536]{0:T(1024)S(1)} %add_rsqrt_fusion.1, f32[1536]{0:T(1024)S(1)} %broadcast_multiply_fusion.4), kind=kOutput, calls=%fused_computation.143 | convolution fusion | flops 7253655552 | bytes 28329984 | tf_op jit(solution)/shard_map/dot_general | solution.py:13
  275.2 49.7 %fusion.85 = f32[1536,768]{1,0:T(8,128)S(1)} fusion(bf16[3072,768]{1,0:T(8,128)(2,1)S(1)} %bitcast.305, f32[1536,3072]{1,0:T(8,128)} %fusion.96), kind=kOutput, calls=%fused_computation.110 | convolution fusion | flops 7554465792 | bytes 28311552 | tf_op jit(solution)/shard_map/dot_general | solution.py:13
  341.0 25.4 %multiply_reduce_fusion.1 = (f32[768]{0:T(1024)}, f32[1536]{0:T(1024)}, f32[1536]{0:T(1024)}, f32[768]{0:T(1024)}, f32[1536,768]{1,0:T(8,128)}) fusion(f32[1536,768]{1,0:T(8,128)} %copy-done.10, f32[1536]{0:T(1024)S(1)} %add_rsqrt_fusion.1, f32[1536]{0:T(1024)S(1)} %broadcast_multiply_fusion.4, f32[768]{0:T(1024)} %param.34, f32[1536,768]{1,0:T(8,128)} %copy-done.4, ...), kind=kOutput, calls=%fused_computation.122 | convolution fusion | flops 14554491904 | bytes 44860416 | tf_op jit(solution)/shard_map/dot_general | solution.py:17
  375.5 6.4 convolution_convert_fusion
  391.5 106.8 %while.31 = (s32[]{:T(128)}, bf16[3,4,128,12,64]{2,4,3,1,0:T(8,128)(2,1)}, bf16[3,4,4,128,12,64]{3,5,2,4,1,0:T(8,128)(2,1)}, bf16[3,4,4,128,12,64]{3,5,4,2,1,0:T...) while((s32[]{:T(128)}, ...), condition=%wide.region_17.18_spmd.clone, body=%wide.region_15.17_spmd.sunk.clone | while | flops 2466662400 | bytes 130804952 | solution.py:192
  398.6 8.7 %select_convert_fusion.3 = (bf16[4,12,128,4,128]{4,2,3,1,0:T(8,128)(2,1)S(1)}, f32[4,12,128,4,128]{4,2,3,1,0:T(8,128)}) fusion(f32[4,12,128,4]{2,3,1,0:T(4,128)S(1)} %dynamic-slice_bitcast_fusion.13, pred[4,4,128]{2,1,0:T(4,128)(4,1)S(1)} %dynamic-slice_bitcast_fusion.14, bf16[3,4,4,128,12,64]{3,5,2,4,1,0:T(8,128)(2,1)} %get-tuple-element.519, ...), kind=kOutput, calls=%fused_computation.33.clone.1.clone | convolution fusion | flops 418381824 | bytes 22907904 | tf_op jit(solution)/shard_map/while/body/eval_jaxpr/gqhd,gnkhd->ghqnk/dot_general | solution.py:82
  407.2 8.1 multiply_convert_fusion.10
  434.0 8.7 %select_convert_fusion.3 = (bf16[4,12,128,4,128]{4,2,3,1,0:T(8,128)(2,1)S(1)}, f32[4,12,128,4,128]{4,2,3,1,0:T(8,128)}) fusion(f32[4,12,128,4]{2,3,1,0:T(4,128)S(1)} %dynamic-slice_bitcast_fusion.13, pred[4,4,128]{2,1,0:T(4,128)(4,1)S(1)} %dynamic-slice_bitcast_fusion.14, bf16[3,4,4,128,12,64]{3,5,2,4,1,0:T(8,128)(2,1)} %get-tuple-element.519, ...), kind=kOutput, calls=%fused_computation.33.clone.1.clone | convolution fusion | flops 418381824 | bytes 22907904 | tf_op jit(solution)/shard_map/while/body/eval_jaxpr/gqhd,gnkhd->ghqnk/dot_general | solution.py:82
  442.7 8.1 multiply_convert_fusion.10
  469.4 8.7 %select_convert_fusion.3 = (bf16[4,12,128,4,128]{4,2,3,1,0:T(8,128)(2,1)S(1)}, f32[4,12,128,4,128]{4,2,3,1,0:T(8,128)}) fusion(f32[4,12,128,4]{2,3,1,0:T(4,128)S(1)} %dynamic-slice_bitcast_fusion.13, pred[4,4,128]{2,1,0:T(4,128)(4,1)S(1)} %dynamic-slice_bitcast_fusion.14, bf16[3,4,4,128,12,64]{3,5,2,4,1,0:T(8,128)(2,1)} %get-tuple-element.519, ...), kind=kOutput, calls=%fused_computation.33.clone.1.clone | convolution fusion | flops 418381824 | bytes 22907904 | tf_op jit(solution)/shard_map/while/body/eval_jaxpr/gqhd,gnkhd->ghqnk/dot_general | solution.py:82
  478.1 8.1 multiply_convert_fusion.10
  498.4 12.3 %copy.105 = bf16[3,4,4,128,12,64]{3,2,5,4,1,0:T(4,128)(2,1)} copy(bf16[3,4,4,128,12,64]{3,5,4,2,1,0:T(8,128)(2,1)} %get-tuple-element.123) | data formatting | bytes 18874368 | tf_op jit(solution)/shard_map/convert_element_type | solution.py:203
  510.6 14.6 %convert_element_type.156 = bf16[12,512,768]{1,2,0:T(8,128)(2,1)} reshape(bf16[3,4,4,128,12,64]{3,2,5,4,1,0:T(4,128)(2,1)} %copy.105) | data formatting | bytes 18874368 | tf_op jit(solution)/shard_map/convert_element_type | solution.py:203
  525.2 16.4 %copy.114 = bf16[12,512,768]{2,0,1:T(8,128)(2,1)} copy(bf16[12,512,768]{1,2,0:T(8,128)(2,1)} %convert_element_type.156) | data formatting | bytes 18874368
  541.6 13.1 %copy.132 = bf16[64,8,12,768]{3,1,2,0:T(8,128)(2,1)} copy(bf16[64,8,12,768]{3,2,1,0:T(8,128)(2,1)} %bitcast.282) | data formatting | bytes 18874368
  554.8 12.3 %copy.103 = bf16[3,4,4,128,12,64]{3,2,5,4,1,0:T(4,128)(2,1)} copy(bf16[3,4,4,128,12,64]{3,5,2,4,1,0:T(8,128)(2,1)} %get-tuple-element.122) | data formatting | bytes 18874368 | tf_op jit(solution)/shard_map/convert_element_type | solution.py:200
  567.1 15.1 %convert_element_type.153 = bf16[12,512,768]{1,2,0:T(8,128)(2,1)} reshape(bf16[3,4,4,128,12,64]{3,2,5,4,1,0:T(4,128)(2,1)} %copy.103) | data formatting | bytes 18874368 | tf_op jit(solution)/shard_map/convert_element_type | solution.py:200
  582.2 16.4 %copy.112 = bf16[12,512,768]{2,0,1:T(8,128)(2,1)} copy(bf16[12,512,768]{1,2,0:T(8,128)(2,1)} %convert_element_type.153) | data formatting | bytes 18874368
  598.5 13.5 %copy.131 = bf16[64,8,12,768]{3,1,2,0:T(8,128)(2,1)} copy(bf16[64,8,12,768]{3,2,1,0:T(8,128)(2,1)} %bitcast.283) | data formatting | bytes 18874368
  622.1 39.5 %all-reduce = (f32[768]{0:T(1024)}, f32[768]{0:T(1024)}, f32[768]{0:T(1024)}, f32[768]{0:T(1024)}) all-reduce(f32[768]{0:T(1024)S(1)} %copy-done.39, f32[768]{0:T(1024)S(1)} %copy-done.40, f32[768]{0:T(1024)S(1)} %copy-done.36, f32[768]{0:T(1024)S(1)} %copy-done.37), channel_id=1, replica_groups=mesh['dp'=8,'seq'=4] {'dp','seq'}, use_global_device_ids=true, to_apply=%region_25.26 | all-reduce | flops 3072 | bytes 24576 | tf_op jit(solution)/shard_map/psum | solution.py:215
  685.8 28.6 %reduce-scatter.7.cloned.1.call-done = bf16[128,9216]{1,0:T(8,128)(2,1)} async-done(((bf16[512,9216]{1,0:T(8,128)(2,1)}), bf16[128,9216]{1,0:T(8,128)(2,1)}) %reduce-scatter.7.cloned.1.call-update) | async-done | bytes 2359312
  729.3 120.3 %all-reduce.4.cloned.1.call-done = (f32[768,64]{0,1:T(8,128)}, f32[64,768]{1,0:T(8,128)}, f32[768,64]{0,1:T(8,128)}, f32[64,768]{1,0:T(8,128)}) async-done(((f32[768,64]{0,1:T(8,128)}, f32[64,768]{1,0:T(8,128)}, f32[768,64]{0,1:T(8,128)}, f32[64,768]{1,0:T(8,128)}), (f32[768,64]{0,1:T(8,128)}, f32[64,768]{1,0:T(8,128)}, f32[768,64]{0,1:T(8,128)}, f32[64,768]{1,0:T(8,128)})) %all-reduce.4.cloned.1.call-update) | async-done | bytes 786448 | tf_op jit(solution)/shard_map/psum | solution.py:215
  (262 shorter events, 245.6 us)
Async XLA Ops:
  7.2 246.9 %copy-start = (bf16[768,768]{1,0:T(8,128)(2,1)S(1)}, bf16[768,768]{1,0:T(8,128)(2,1)}, u32[]{:S(2)}) copy-start(bf16[768,768]{1,0:T(8,128)(2,1)} %param.27) | copy-start | bytes 3538948
  7.2 74.8 %all-gather.5.cloned.1.call-start = ((), (), s32[]{:S(2)}) async-start(), calls=%async_computation.3 | async-start | bytes 11796480 | tf_op jit(solution)/shard_map/all_gather | solution.py:143
  13.8 135.8 %all-gather.3.cloned.1.call-start = ((), (), s32[]{:S(2)}) async-start(), calls=%async_computation.2 | async-start | bytes 11796480 | tf_op jit(solution)/shard_map/all_gather | solution.py:144
  20.3 658.0 %reduce-scatter.9.cloned.1.call-start = ((), (), s32[]{:S(2)}) async-start(), calls=%async_computation.5 | async-start | bytes 11796480
  242.0 7.0 copy-start.2
  242.0 7.0 copy-start.27
  259.0 16.2 %slice-start.8 = ((s8[4718592]{0:T(1024)(128)(4,1)}), s8[4194304]{0:T(1024)(128)(4,1)S(1)}, s32[]{:S(2)}) async-start(s8[4718592]{0:T(1024)(128)(4,1)} %bitcast.304), calls=%async_computation.15 | async-start | bytes 8388608
  261.0 64.8 %copy-start.10 = (f32[1536,768]{1,0:T(8,128)}, f32[1536,768]{1,0:T(8,128)S(1)}, u32[]{:S(2)}) copy-start(f32[1536,768]{1,0:T(8,128)S(1)} %get-tuple-element.271) | copy-start | bytes 14155780
  264.2 11.0 %slice-start.9 = ((s8[4718592]{0:T(1024)(128)(4,1)}), s8[524288]{0:T(1024)(128)(4,1)S(1)}, s32[]{:S(2)}) async-start(s8[4718592]{0:T(1024)(128)(4,1)} %bitcast.304), calls=%async_computation.16 | async-start | bytes 1048576
  275.2 49.7 %copy-start.26 = (bf16[768,64]{0,1:T(8,128)(2,1)S(1)}, bf16[768,64]{0,1:T(8,128)(2,1)}, u32[]{:S(2)}) copy-start(bf16[768,64]{0,1:T(8,128)(2,1)} %param.32) | copy-start | bytes 294916
  327.1 10.3 %copy-start.21 = (f32[1536,64]{0,1:T(8,128)}, f32[1536,64]{0,1:T(8,128)S(1)}, u32[]{:S(2)}) copy-start(f32[1536,64]{0,1:T(8,128)S(1)} %fusion.112) | copy-start | bytes 1179652
  367.1 6.8 copy-start.19
  367.1 6.8 copy-start.30
  381.8 9.7 %copy-start.3 = (bf16[3,4,128,12,64]{2,4,3,1,0:T(8,128)(2,1)S(1)}, bf16[3,4,128,12,64]{2,4,3,1,0:T(8,128)(2,1)}, u32[]{:S(2)}) copy-start(bf16[3,4,128,12,64]{2,4,3,1,0:T(8,128)(2,1)} %copy-done.2) | copy-start | bytes 7077892
  407.2 8.1 copy-start.11
  442.7 8.1 copy-start.11
  478.1 8.1 copy-start.11
  554.8 159.6 %reduce-scatter.7.cloned.1.call-start = ((), (), s32[]{:S(2)}) async-start(), calls=%async_computation.4 | async-start | bytes 11796480
  612.0 237.5 %all-reduce.4.cloned.1.call-start = ((), (), s32[]{:S(2)}) async-start(), calls=%async_computation.6 | async-start | bytes 1572864 | tf_op jit(solution)/shard_map/psum | solution.py:215
  613.7 8.3 copy-start.36
  613.7 8.3 copy-start.37
  613.7 8.3 copy-start.39
  613.7 8.3 copy-start.40
  613.7 47.8 %copy-start.17 = (bf16[1536,64]{0,1:T(8,128)(2,1)S(1)}, bf16[1536,64]{0,1:T(8,128)(2,1)}, u32[]{:S(2)}) copy-start(bf16[1536,64]{0,1:T(8,128)(2,1)} %copy-done.16) | copy-start | bytes 589828
  616.9 48.3 %copy-start.25 = (bf16[1536,64]{0,1:T(8,128)(2,1)S(1)}, bf16[1536,64]{0,1:T(8,128)(2,1)}, u32[]{:S(2)}) copy-start(bf16[1536,64]{0,1:T(8,128)(2,1)} %copy-done.24) | copy-start | bytes 589828
  622.0 46.9 %slice-start = ((s8[4718592]{0:T(1024)(128)(4,1)}), s8[524288]{0:T(1024)(128)(4,1)S(1)}, s32[]{:S(2)}) async-start(s8[4718592]{0:T(1024)(128)(4,1)} %bitcast.284), calls=%async_computation.7 | async-start | bytes 1048576
  661.5 7.4 slice-start.1
  661.5 7.4 copy-start.22
  665.2 5.6 slice-start.2
  685.8 36.4 %copy-start.44 = (bf16[768,768]{1,0:T(8,128)(2,1)S(1)}, bf16[768,768]{1,0:T(8,128)(2,1)}, u32[]{:S(2)}) copy-start(bf16[768,768]{1,0:T(8,128)(2,1)} %param.25) | copy-start | bytes 3538948
  719.4 4.9 slice-start.4
  724.6 131.4 %copy-start.1 = (bf16[768,768]{1,0:T(8,128)(2,1)S(1)}, bf16[768,768]{1,0:T(8,128)(2,1)}, u32[]{:S(2)}) copy-start(bf16[768,768]{1,0:T(8,128)(2,1)} %param.27) | copy-start | bytes 3538948
  (37 other events, 94.6 us)
Sparse Core Ops, SparseCore 0:
  13.9 67.9 all-gather.4
  84.1 65.4 all-gather.2
  554.9 78.5 reduce-scatter.8
  635.9 78.4 reduce-scatter.6
  720.5 129.0 all-reduce.3
where the time goes:
time: 874 us; the launch traced here: 863 us
  matrix products  264 us (30%)
  local copies, waits for them, and re-layouts  249 us (28%)
  waiting for transfers between devices  235 us (27%)
  other arithmetic  59.3 us (7%)
  blocking collectives  39.5 us (5%)
  between operations  14.7 us (2%)
    psum x1, waiting for transfers between devices, per_device(): lax.psum((grad_down_one, grad_up_one, grad_down_two, grad_up_two, grad_ga...  120 us
    unnamed x120, local copies, waits for them, and re-layouts  87.2 us
    dot_general x10, matrix products, matmul(): return jnp.dot(left, right, preferred_element_type=jnp.float32)  84.3 us
    dot_general x8, matrix products, matmul_rt(): lax.dot_general(left, right, (((1,), (1,)), ((), ())), preferred_element_...  46.6 us
    all_gather x1, waiting for transfers between devices, per_device(): lax.all_gather(key_own, 'seq', axis=1, tiled=True)  43.6 us
    all_gather x1, waiting for transfers between devices, per_device(): lax.all_gather(value_own, 'seq', axis=1, tiled=True)  42.8 us
    psum x1, blocking collectives, per_device(): lax.psum((grad_down_one, grad_up_one, grad_down_two, grad_up_two, grad_ga...  39.5 us
    unnamed x7, waiting for transfers between devices  28.7 us
  transfers between devices with their start and end apart: 5, of which 4 were waited for; matrix products, arithmetic and copies ran while one was open for 18% of the time, Pallas kernels for 0%

commit v1 on v0

v1 whole, which is shorter than its diff:
```python
import functools

import jax
import jax.numpy as jnp
from jax import lax
from jax.experimental import pallas as pl
from jax.experimental.pallas import tpu as pltpu
from jax.sharding import PartitionSpec as P

HEADS = 12
EPS = 1e-06
F32 = jnp.float32
BF16 = jnp.bfloat16
NN = (((1,), (0,)), ((), ()))
NT = (((1,), (1,)), ((), ()))
TN = (((0,), (0,)), ((), ()))
MESH = pl.DeviceIdType.MESH
LANES = 128
GROUP = 8


def dot(left, right, dims=NN):
    return lax.dot_general(left, right, dims, preferred_element_type=F32)


def gelu_parts(value):
    phi = 0.5 + 0.5 * lax.erf(value * 0.7071067811865476)
    scaled = value * jnp.exp(value * value * -0.5) * 0.3989422804014327
    return value * phi, phi + scaled


def row_mean(value):
    return jnp.sum(value, axis=-1, keepdims=True) * (1.0 / value.shape[-1])


def norm_forward(hidden):
    centred = hidden - row_mean(hidden)
    inverse = lax.rsqrt(row_mean(centred * centred) + EPS)
    return centred * inverse, inverse


def norm_backward(grad, unit, inverse, gain):
    scaled = grad * gain
    inner = scaled - row_mean(scaled) - unit * row_mean(scaled * unit)
    return inner * inverse


class Refs:
    pass


def attend_forward(s, bias):
    span = s.query.shape[1]
    half = span // 2
    low = lax.broadcasted_iota(jnp.int32, (1, LANES), 1) < LANES // 2

    @pl.loop(0, s.query.shape[0])
    def _(pair):
        key, value = s.key[pair], s.value[pair]
        zero = jnp.zeros_like(key)
        keys = (jnp.where(low, key, zero), jnp.where(low, zero, key))
        for block in range(2):
            rows = pl.ds(block * half, half)
            query = s.query[pair, rows, :]
            outs, invs = [], []
            for head in range(2):
                scores = dot(query, keys[head], NT) + bias
                top = jnp.max(scores, axis=-1, keepdims=True)
                expo = jnp.exp(scores - top)
                total = jnp.sum(expo, axis=-1, keepdims=True)
                expo_low = expo.astype(BF16)
                s.expo[2 * pair + head, rows, :] = expo_low
                outs.append(dot(expo_low, value))
                invs.append(1.0 / total)
            inv = jnp.where(low, invs[0], invs[1])
            attn = jnp.where(low, outs[0], outs[1]) * inv
            s.inv[pair, rows, :] = inv
            s.attn[pair, rows, :] = attn
            s.ctx[rows, pl.ds(pl.multiple_of(pair * LANES, LANES), LANES)] = attn.astype(BF16)


def attend_backward(s):
    span = s.query.shape[1]
    half = span // 2
    low = lax.broadcasted_iota(jnp.int32, (1, LANES), 1) < LANES // 2

    @pl.loop(0, s.query.shape[0])
    def _(pair):
        lanes = pl.ds(pl.multiple_of(pair * LANES, LANES), LANES)
        key, value, query = s.key[pair], s.value[pair], s.query[pair]
        zero = jnp.zeros_like(key)
        keys = (jnp.where(low, key, zero), jnp.where(low, zero, key))
        wide = s.ctx[:, lanes].astype(F32) * s.inv[pair]
        terms = wide * s.attn[pair]
        deltas = (
            jnp.sum(jnp.where(low, terms, 0.0), axis=-1, keepdims=True),
            jnp.sum(jnp.where(low, 0.0, terms), axis=-1, keepdims=True),
        )
        grad = wide.astype(BF16)
        grads = (jnp.where(low, grad, zero), jnp.where(low, zero, grad))
        grad_t, query_t = grad.T, query.T
        dquery = [None, None]
        for head in range(2):
            sub = slice(head * LANES // 2, (head + 1) * LANES // 2)
            for block in range(2):
                rows = slice(block * half, (block + 1) * half)
                expo = s.expo[2 * pair + head, pl.ds(block * half, half), :]
                dprob = dot(grads[head][rows], value, NT)
                dscores = (expo.astype(F32) * (dprob - deltas[head][rows])).astype(BF16)
                s.dscores[head, pl.ds(block * half, half), :] = dscores
                part = dot(dscores, keys[head])
                dquery[block] = part if head == 0 else dquery[block] + part
            s.dvalue_t[sub, :] = dot(grad_t[sub], s.expo[2 * pair + head]).astype(BF16)
            s.dkey_t[sub, :] = dot(query_t[sub], s.dscores[head]).astype(BF16)
        scale = (LANES // 2) ** -0.5
        for block in range(2):
            s.dquery[pl.ds(block * half, half), lanes] = (dquery[block] * scale).astype(BF16)
        s.dkey[:, lanes] = s.dkey_t[...].T
        s.dvalue[:, lanes] = s.dvalue_t[...].T


def layer(s, tokens, cotangent, length, before_dy):
    span, width = tokens.shape
    pairs = width // LANES
    tiles = s.w_inner.shape[0]
    block = 256
    blocks = span // block
    scale = (LANES // 2) ** -0.5

    for b in range(blocks):
        rows = pl.ds(b * block, block)
        x = tokens[rows, :]
        for weight, target, factor in (
            (s.w_query, s.query, scale),
            (s.w_key, s.key, None),
            (s.w_value, s.value, None),
        ):
            y = dot(x, weight[...]).astype(BF16)
            if factor is not None:
                y = y * jnp.asarray(factor, BF16)
            for pair in range(pairs):
                target[pair, rows, :] = y[:, pair * LANES : (pair + 1) * LANES]

    position = lax.broadcasted_iota(jnp.int32, (1, span), 1)
    bias = jnp.where(position < length, 0.0, -1e30)
    attend_forward(s, bias)

    for b in range(blocks):
        rows = pl.ds(b * block, block)
        out = dot(s.ctx[rows, :], s.w_out[...])
        out_low = out.astype(BF16)
        s.out_low[rows, :] = out_low
        act, slope = gelu_parts(dot(out_low, s.down_one[...]))
        act = act.astype(BF16)
        s.act_one[rows, :] = act
        s.slope_one[rows, :] = slope
        hidden = tokens[rows, :].astype(F32) + out + dot(act, s.up_one[...])
        unit, inverse = norm_forward(hidden)
        s.unit_one[rows, :] = unit
        s.inverse_one[rows, :] = inverse
        normed = unit * s.gain_one[...] + s.bias_one[...]
        s.normed_low[rows, :] = normed.astype(BF16)
        s.total[rows, :] = jnp.zeros((block, width), F32)

    @pl.loop(0, tiles)
    def _(tile):
        for b in range(blocks):
            rows = pl.ds(b * block, block)
            act, slope = gelu_parts(dot(s.normed_low[rows, :], s.w_inner[tile]))
            s.slope[tile, rows, :] = slope.astype(BF16)
            s.total[rows, :] += dot(act.astype(BF16), s.w_outer[tile])

    before_dy()
    for b in range(blocks):
        rows = pl.ds(b * block, block)
        ffn = s.total[rows, :]
        ffn_low = ffn.astype(BF16)
        act, slope = gelu_parts(dot(ffn_low, s.down_two[...]))
        act = act.astype(BF16)
        normed = s.unit_one[rows, :] * s.gain_one[...] + s.bias_one[...]
        hidden = normed + ffn + dot(act, s.up_two[...])
        unit, inverse = norm_forward(hidden)
        s.output[rows, :] = (unit * s.gain_two[...] + s.bias_two[...]).astype(BF16)
        dy = cotangent[rows, :].astype(F32)
        s.vectors[2:3, :] += jnp.sum(dy * unit, axis=0, keepdims=True)
        s.vectors[3:4, :] += jnp.sum(dy, axis=0, keepdims=True)
        dh = norm_backward(dy, unit, inverse, s.gain_two[...])
        da = dh.astype(BF16)
        s.grads[3] += dot(act, da, TN)
        dz = (dot(da, s.up_two[...], NT) * slope).astype(BF16)
        s.grads[2] += dot(dz, ffn_low, TN)
        s.total[rows, :] = dh
        s.dffn[rows, :] = (dh + dot(dz, s.down_two[...], NT)).astype(BF16)

    @pl.loop(0, tiles)
    def _(tile):
        for b in range(blocks):
            rows = pl.ds(b * block, block)
            du = dot(s.dffn[rows, :], s.w_outer[tile], NT) * s.slope[tile, rows, :].astype(F32)
            s.total[rows, :] += dot(du.astype(BF16), s.w_inner[tile], NT)

    for b in range(blocks):
        rows = pl.ds(b * block, block)
        dy = s.total[rows, :]
        unit = s.unit_one[rows, :]
        s.vectors[0:1, :] += jnp.sum(dy * unit, axis=0, keepdims=True)
        s.vectors[1:2, :] += jnp.sum(dy, axis=0, keepdims=True)
        dh = norm_backward(dy, unit, s.inverse_one[rows, :], s.gain_one[...])
        s.total[rows, :] = dh
        da = dh.astype(BF16)
        s.grads[1] += dot(s.act_one[rows, :], da, TN)
        dz = (dot(da, s.up_one[...], NT) * s.slope_one[rows, :]).astype(BF16)
        s.grads[0] += dot(dz, s.out_low[rows, :], TN)
        dout = (dh + dot(dz, s.down_one[...], NT)).astype(BF16)
        s.ctx[rows, :] = dot(dout, s.w_out[...], NT).astype(BF16)

    attend_backward(s)

    for b in range(blocks):
        rows = pl.ds(b * block, block)
        grad = s.total[rows, :] + dot(s.dquery[rows, :], s.w_query[...], NT)
        grad = grad + dot(s.dkey[rows, :], s.w_key[...], NT)
        grad = grad + dot(s.dvalue[rows, :], s.w_value[...], NT)
        s.grad_in[rows, :] = grad.astype(BF16)


INPUTS = (
    "w_query", "w_key", "w_value", "w_out", "w_inner", "w_outer",
    "down_one", "up_one", "down_two", "up_two",
    "gain_one", "bias_one", "gain_two", "bias_two",
)
BIG = INPUTS[:6]


def layer_scratch(span, width, hidden, adapt):
    pairs, tiles = width // LANES, hidden // width
    v = pltpu.VMEM
    return {
        "w_query": v((width, width), BF16),
        "w_key": v((width, width), BF16),
        "w_value": v((width, width), BF16),
        "w_out": v((width, width), BF16),
        "w_inner": v((tiles, width, width), BF16),
        "w_outer": v((tiles, width, width), BF16),
        "query": v((pairs, span, LANES), BF16),
        "key": v((pairs, span, LANES), BF16),
        "value": v((pairs, span, LANES), BF16),
        "expo": v((2 * pairs, span, span), BF16),
        "inv": v((pairs, span, LANES), F32),
        "attn": v((pairs, span, LANES), F32),
        "ctx": v((span, width), BF16),
        "out_low": v((span, width), BF16),
        "act_one": v((span, adapt), BF16),
        "slope_one": v((span, adapt), F32),
        "unit_one": v((span, width), F32),
        "inverse_one": v((span, 1), F32),
        "normed_low": v((span, width), BF16),
        "slope": v((tiles, span, width), BF16),
        "total": v((span, width), F32),
        "dffn": v((span, width), BF16),
        "dscores": v((2, span, span), BF16),
        "dvalue_t": v((LANES, span), BF16),
        "dkey_t": v((LANES, span), BF16),
        "dquery": v((span, width), BF16),
        "dkey": v((span, width), BF16),
        "dvalue": v((span, width), BF16),
    }


def layer_kernel(parts, per, lengths, tokens, cotangent, *refs):
    s = Refs()
    refs = list(refs)
    for name in INPUTS:
        setattr(s, name, refs.pop(0))
    hbm = {name: getattr(s, name) for name in BIG}
    output, grad_in, grads, vectors = (refs.pop(0) for _ in range(4))
    s.grads, s.vectors = grads, vectors
    names = list(layer_scratch(2 * LANES, 2 * LANES, 2 * LANES, 8))
    for name in names:
        setattr(s, name, refs.pop(0))
    x_in, dy_in, out_buf, grad_buf, w_sem, own_sem, send_sem, recv_sem = refs

    me = lax.axis_index("seq")
    rows = tokens.shape[1]
    mine = pl.ds(me * rows, rows)
    peers = [lax.rem(me + p, parts) for p in range(parts)]
    sources = [lax.rem(me + parts - p, parts) for p in range(parts)]

    barrier = pltpu.get_barrier_semaphore()
    for p in range(1, parts):
        pl.semaphore_signal(barrier, inc=1, device_id={"seq": peers[p]}, device_id_type=MESH)

    width = tokens.shape[2]
    weight_copies = []
    for index, name in enumerate(BIG):
        ref = getattr(s, name)
        if name == "w_inner":
            for t in range(ref.shape[0]):
                weight_copies.append(
                    pltpu.make_async_copy(hbm[name].at[:, pl.ds(t * width, width)], ref.at[t], w_sem.at[index, t])
                )
        elif name == "w_outer":
            for t in range(ref.shape[0]):
                weight_copies.append(
                    pltpu.make_async_copy(hbm[name].at[pl.ds(t * width, width), :], ref.at[t], w_sem.at[index, t])
                )
        else:
            weight_copies.append(pltpu.make_async_copy(hbm[name], ref, w_sem.at[index, 0]))
    for copy in weight_copies:
        copy.start()

    pl.semaphore_wait(barrier, parts - 1)

    def inbound(array, step, p):
        source, target = ((tokens, x_in), (cotangent, dy_in))[array]
        if p == 0:
            return pltpu.make_async_copy(
                source.at[step * parts + me], target.at[step, mine], own_sem.at[array, step]
            )
        return pltpu.make_async_remote_copy(
            src_ref=source.at[step * parts + peers[p]],
            dst_ref=target.at[step, mine],
            send_sem=send_sem.at[array, step, p],
            recv_sem=recv_sem.at[array, step, p],
            device_id={"seq": peers[p]},
            device_id_type=MESH,
        )

    def outbound(array, step, p):
        source, target = ((out_buf, output), (grad_buf, grad_in))[array - 2]
        block = source.at[step, pl.ds(peers[p] * rows, rows)]
        if p == 0:
            return pltpu.make_async_copy(block, target.at[step * parts + me], own_sem.at[array, step])
        return pltpu.make_async_remote_copy(
            src_ref=block,
            dst_ref=target.at[step * parts + me],
            send_sem=send_sem.at[array, step, p],
            recv_sem=recv_sem.at[array, step, p],
            device_id={"seq": peers[p]},
            device_id_type=MESH,
        )

    def start(make, array, step):
        for p in [*range(1, parts), 0]:
            make(array, step, p).start()

    def finish(make, array, step):
        for p in range(parts):
            make(array, step, p).wait()

    start(inbound, 0, 0)
    for ref in (grads, vectors):
        ref[...] = jnp.zeros_like(ref)
    for copy in weight_copies:
        copy.wait()

    @pl.loop(0, per)
    def _(step):
        finish(inbound, 0, step)
        start(inbound, 1, step)

        @pl.when(step + 1 < per)
        def _():
            start(inbound, 0, step + 1)

        s.output, s.grad_in = out_buf.at[step], grad_buf.at[step]
        layer(
            s,
            x_in.at[step],
            dy_in.at[step],
            lengths[step * parts + me],
            lambda: finish(inbound, 1, step),
        )
        start(outbound, 2, step)
        start(outbound, 3, step)

    @pl.loop(0, per)
    def _(step):
        finish(outbound, 2, step)
        finish(outbound, 3, step)


def per_device(parts, tokens, lengths, cotangent, *params):
    batch, rows, width = tokens.shape
    hidden, adapt = params[4].shape[1], params[6].shape[1]
    per, span = batch // parts, parts * rows
    params = [p.reshape(1, width) if p.ndim == 1 else p for p in params]
    vmem = pl.BlockSpec(memory_space=pltpu.VMEM)
    anywhere = pl.BlockSpec(memory_space=pl.ANY)
    dma = pltpu.SemaphoreType.DMA
    output, grad_in, grads, vectors = pl.pallas_call(
        functools.partial(layer_kernel, parts, per),
        out_shape=(
            jax.ShapeDtypeStruct((batch, rows, width), BF16),
            jax.ShapeDtypeStruct((batch, rows, width), BF16),
            jax.ShapeDtypeStruct((4, adapt, width), F32),
            jax.ShapeDtypeStruct((8, width), F32),
        ),
        in_specs=[pl.BlockSpec(memory_space=pltpu.SMEM)]
        + [anywhere] * 2
        + [anywhere if name in BIG else vmem for name in INPUTS],
        out_specs=(anywhere, anywhere, vmem, vmem),
        scratch_shapes=list(layer_scratch(span, width, hidden, adapt).values())
        + [pltpu.VMEM((per, span, width), BF16)] * 4
        + [dma((6, hidden // width)), dma((4, per)), dma((4, per, parts)), dma((4, per, parts))],
        compiler_params=pltpu.CompilerParams(
            collective_id=0, has_side_effects=True, vmem_limit_bytes=62 * 2**20
        ),
        name="layer",
    )(lengths, tokens, cotangent, *params)
    down_one, up_one, down_two, up_two, sums = lax.psum(
        (grads[0], grads[1], grads[2], grads[3], vectors), ("dp", "seq")
    )
    return (
        output,
        grad_in.astype(F32),
        down_one.T,
        up_one,
        down_two.T,
        up_two,
        sums[0],
        sums[1],
        sums[2],
        sums[3],
    )


def solution(mesh):
    split = P("dp", "seq", None)
    return jax.shard_map(
        functools.partial(per_device, mesh.shape["seq"]),
        mesh=mesh,
        in_specs=(split, P("dp"), split) + (P(),) * 14,
        out_specs=(split, split) + (P(),) * 8,
        check_vma=False,
    )
```

time: 874 us -> 333 us (0.38)
  matrix products: 264 us -> 0 us
  local copies, waits for them, and re-layouts: 249 us -> 17.4 us
  Pallas kernels: 0 us -> 170 us
  waiting for transfers between devices: 235 us -> 87.7 us
  other arithmetic: 59.3 us -> 2.65 us
    dot_general x46 -> x0, matrix products: 264 us -> none  [the longest x10 84.3 us: matmul(): return jnp.dot(left, right, preferred_element_type=jnp.float32)]
    pallas_call x0 -> x1, Pallas kernels: none -> 170 us  [per_device(): pl.pallas_call(functools.partial(layer_kernel, parts, per), out_shape=(ja...]
    all_gather x2 -> x0, waiting for transfers between devices: 86.4 us -> none  [the longest x1 43.6 us: per_device(): lax.all_gather(key_own, 'seq', axis=1, tiled=True)]
    convert_element_type x10 -> x0, local copies, waits for them, and re-layouts: 78.6 us -> none  [the longest x2 27.4 us: per_device(): key_terms.astype(jnp.bfloat16)]
    unnamed x120 -> x19, local copies, waits for them, and re-layouts: 87.2 us -> 9.44 us
    reshape x6 -> x4, local copies, waits for them, and re-layouts: 40.5 us -> 5.07 us  [per_device(): params = [p.reshape(1, width) if p.ndim == 1 else p for p in params]]
    psum x1, waiting for transfers between devices: 120 us -> 87.6 us  [per_device(): lax.psum((grads[0], grads[1], grads[2], grads[3], vectors), ('dp', 'seq'))]
    unnamed x7 -> x1, waiting for transfers between devices: 28.7 us -> 0.02 us
  transfers between devices with their start and end apart: 5 -> 1, of which waited for: 4 -> 1; matrix products, arithmetic and copies ran while one was open for 18% -> 1% of each run, Pallas kernels for 0% -> 0%
where the time goes in v1:
time: 333 us; the launch traced here: 330 us
  Pallas kernels  170 us (51%)
  waiting for transfers between devices  87.7 us (26%)
  blocking collectives  38.8 us (12%)
  local copies, waits for them, and re-layouts  17.4 us (5%)
  between operations  14.1 us (4%)
    pallas_call x1, Pallas kernels, per_device(): pl.pallas_call(functools.partial(layer_kernel, parts, per), out_shape=(ja...  170 us
    psum x1, waiting for transfers between devices, per_device(): lax.psum((grads[0], grads[1], grads[2], grads[3], vectors), ('dp', 'seq'))  87.6 us
    psum x1, blocking collectives, per_device(): lax.psum((grads[0], grads[1], grads[2], grads[3], vectors), ('dp', 'seq'))  38.8 us
    unnamed x19, local copies, waits for them, and re-layouts  9.44 us
  transfers between devices with their start and end apart: 1, of which 1 were waited for; matrix products, arithmetic and copies ran while one was open for 1% of the time, Pallas kernels for 0%

profile of v1, /device:TPU:1, one launch (start us, length us, event | category | flops | bytes accessed | tf_op | source)
XLA Modules:
  0.0 330.5 jit_solution(12602093751830118446)
XLA Ops:
  7.2 0.0 all-reduce.3.cloned.1.call-start
  7.2 1.3 reshape.32.refs_10_
  8.5 1.3 reshape.33.refs_11_
  9.8 1.3 reshape.34.refs_12_
  11.0 1.3 reshape.35.refs_13_
  12.3 1.7 copy.27.refs_6_
  14.0 1.7 copy.28.refs_8_
  15.7 169.9 %layer.1 = (bf16[12,128,768]{2,1,0:T(8,128)(2,1)}, bf16[12,128,768]{2,1,0:T(8,128)(2,1)}, f32[4,64,768]{2,1,0:T(8,128)}, f32[8,768]{1,0:T(8,128)}) custom-call(s32[12]{0:T(128)} %lengths.1, bf16[12,128,768]{2,1,0:T(8,128)(2,1)} %tokens.1, bf16[12,128,768]{2,1,0:T(8,128)(2,1)} %cotangent.1, bf16[768,768]{1,0:T(8,128)(2,1)} %refs_0_.1, ...), custom_call_target="tpu_custom_call" | custom-call | tf_op jit(solution)/shard_map/layer/pallas_call | solution.py:391
  185.6 0.0 copy-start
  185.6 2.2 slice_bitcast_fusion
  187.8 0.0 all-reduce.3.cloned.1.call-update
  187.9 0.0 copy-done
  187.9 0.0 copy-start.5
  187.9 2.7 convert_element_type.3
  190.5 0.0 copy-done.5
  190.5 38.8 %psum.39 = f32[8,768]{1,0:T(8,128)S(1)} all-reduce(f32[8,768]{1,0:T(8,128)S(1)} %copy-done.5), channel_id=1, replica_groups=mesh['dp'=8,'seq'=4] {'dp','seq'}, use_global_device_ids=true, to_apply=%region_4.0 | all-reduce | flops 6144 | bytes 49152 | tf_op jit(solution)/shard_map/psum | solution.py:411
  229.4 0.6 slice_reduce_fusion
  230.0 87.6 %all-reduce.3.cloned.1.call-done = (f32[768,64]{0,1:T(8,128)}, f32[64,768]{1,0:T(8,128)}, f32[768,64]{0,1:T(8,128)}, f32[64,768]{1,0:T(8,128)}) async-done(((f32[768,64]{0,1:T(8,128)}, f32[64,768]{1,0:T(8,128)}, f32[768,64]{0,1:T(8,128)}, f32[64,768]{1,0:T(8,128)}), (f32[768,64]{0,1:T(8,128)}, f32[64,768]{1,0:T(8,128)}, f32[768,64]{0,1:T(8,128)}, f32[64,768]{1,0:T(8,128)})) %all-reduce.3.cloned.1.call-update) | async-done | bytes 786448 | tf_op jit(solution)/shard_map/psum | solution.py:411
  317.6 0.0 copy-start.4
  317.6 0.0 copy-start.3
  317.6 0.0 copy-start.2
  317.6 0.0 copy-start.1
  317.6 3.3 copy.34
  320.9 0.0 copy-done.4
  320.9 0.7 copy.35
  321.6 0.0 copy-done.3
  321.6 0.7 copy.36
  322.3 0.0 copy-done.2
  322.3 0.7 copy.37
  323.0 0.0 copy-done.1
  323.0 0.7 copy.38
Async XLA Ops:
  7.2 310.5 %all-reduce.3.cloned.1.call-start = ((), (), s32[]{:S(2)}) async-start(), calls=%async_computation | async-start | bytes 1572864 | tf_op jit(solution)/shard_map/psum | solution.py:411
  185.6 2.3 copy-start
  187.9 2.7 copy-start.5
  317.6 3.3 %copy-start.4 = (f32[768,64]{0,1:T(8,128)S(1)}, f32[768,64]{0,1:T(8,128)}, u32[]{:S(2)}) copy-start(f32[768,64]{0,1:T(8,128)} %get-tuple-element.42) | copy-start | bytes 589828
  317.6 4.0 %copy-start.3 = (f32[64,768]{1,0:T(8,128)S(1)}, f32[64,768]{1,0:T(8,128)}, u32[]{:S(2)}) copy-start(f32[64,768]{1,0:T(8,128)} %get-tuple-element.43) | copy-start | bytes 589828
  317.6 4.7 %copy-start.2 = (f32[768,64]{0,1:T(8,128)S(1)}, f32[768,64]{0,1:T(8,128)}, u32[]{:S(2)}) copy-start(f32[768,64]{0,1:T(8,128)} %get-tuple-element.44) | copy-start | bytes 589828
  317.6 5.3 %copy-start.1 = (f32[64,768]{1,0:T(8,128)S(1)}, f32[64,768]{1,0:T(8,128)}, u32[]{:S(2)}) copy-start(f32[64,768]{1,0:T(8,128)} %get-tuple-element.45) | copy-start | bytes 589828
Sparse Core Ops, SparseCore 0:
  188.0 129.6 all-reduce.2

commit v2 on v1

v2 whole, which is shorter than its diff:
```python
import functools

import jax
import jax.numpy as jnp
from jax import lax
from jax.experimental import pallas as pl
from jax.experimental.pallas import tpu as pltpu
from jax.sharding import PartitionSpec as P

HEADS = 12
EPS = 1e-06
F32 = jnp.float32
BF16 = jnp.bfloat16
NN = (((1,), (0,)), ((), ()))
NT = (((1,), (1,)), ((), ()))
TN = (((0,), (0,)), ((), ()))
MESH = pl.DeviceIdType.MESH
LANES = 128
GROUP = 8


def dot(left, right, dims=NN):
    return lax.dot_general(left, right, dims, preferred_element_type=F32)


def gelu_parts(value):
    phi = 0.5 + 0.5 * lax.erf(value * 0.7071067811865476)
    scaled = value * jnp.exp(value * value * -0.5) * 0.3989422804014327
    return value * phi, phi + scaled


def row_mean(value):
    return jnp.sum(value, axis=-1, keepdims=True) * (1.0 / value.shape[-1])


def norm_forward(hidden):
    centred = hidden - row_mean(hidden)
    inverse = lax.rsqrt(row_mean(centred * centred) + EPS)
    return centred * inverse, inverse


def norm_backward(grad, unit, inverse, gain):
    scaled = grad * gain
    inner = scaled - row_mean(scaled) - unit * row_mean(scaled * unit)
    return inner * inverse


class Refs:
    pass


def attend_forward(s, bias):
    span = s.query.shape[1]
    half = span // 2
    low = lax.broadcasted_iota(jnp.int32, (1, LANES), 1) < LANES // 2

    @pl.loop(0, s.query.shape[0])
    def _(pair):
        key, value = s.key[pair], s.value[pair]
        zero = jnp.zeros_like(key)
        keys = (jnp.where(low, key, zero), jnp.where(low, zero, key))
        for block in range(2):
            rows = pl.ds(block * half, half)
            query = s.query[pair, rows, :]
            outs, invs = [], []
            for head in range(2):
                scores = dot(query, keys[head], NT) + bias
                top = jnp.max(scores, axis=-1, keepdims=True)
                expo = jnp.exp(scores - top)
                total = jnp.sum(expo, axis=-1, keepdims=True)
                expo_low = expo.astype(BF16)
                s.expo[2 * pair + head, rows, :] = expo_low
                outs.append(dot(expo_low, value))
                invs.append(1.0 / total)
            inv = jnp.where(low, invs[0], invs[1])
            attn = jnp.where(low, outs[0], outs[1]) * inv
            s.inv[pair, rows, :] = inv
            s.attn[pair, rows, :] = attn
            s.ctx[rows, pl.ds(pl.multiple_of(pair * LANES, LANES), LANES)] = attn.astype(BF16)


def attend_backward(s, hook=None):
    span = s.query.shape[1]
    half = span // 2
    low = lax.broadcasted_iota(jnp.int32, (1, LANES), 1) < LANES // 2

    @pl.loop(0, s.query.shape[0])
    def _(pair):
        if hook is not None:
            hook(pair)
        lanes = pl.ds(pl.multiple_of(pair * LANES, LANES), LANES)
        key, value, query = s.key[pair], s.value[pair], s.query[pair]
        zero = jnp.zeros_like(key)
        keys = (jnp.where(low, key, zero), jnp.where(low, zero, key))
        wide = s.ctx[:, lanes].astype(F32) * s.inv[pair]
        terms = wide * s.attn[pair]
        deltas = (
            jnp.sum(jnp.where(low, terms, 0.0), axis=-1, keepdims=True),
            jnp.sum(jnp.where(low, 0.0, terms), axis=-1, keepdims=True),
        )
        grad = wide.astype(BF16)
        grads = (jnp.where(low, grad, zero), jnp.where(low, zero, grad))
        grad_t, query_t = grad.T, query.T
        dquery = [None, None]
        for head in range(2):
            sub = slice(head * LANES // 2, (head + 1) * LANES // 2)
            for block in range(2):
                rows = slice(block * half, (block + 1) * half)
                expo = s.expo[2 * pair + head, pl.ds(block * half, half), :]
                dprob = dot(grads[head][rows], value, NT)
                dscores = (expo.astype(F32) * (dprob - deltas[head][rows])).astype(BF16)
                s.dscores[head, pl.ds(block * half, half), :] = dscores
                part = dot(dscores, keys[head])
                dquery[block] = part if head == 0 else dquery[block] + part
            s.dvalue_t[sub, :] = dot(grad_t[sub], s.expo[2 * pair + head]).astype(BF16)
            s.dkey_t[sub, :] = dot(query_t[sub], s.dscores[head]).astype(BF16)
        scale = (LANES // 2) ** -0.5
        for block in range(2):
            s.dquery[pl.ds(block * half, half), lanes] = (dquery[block] * scale).astype(BF16)
        s.dkey[:, lanes] = s.dkey_t[...].T
        s.dvalue[:, lanes] = s.dvalue_t[...].T


BLOCK = 256


def blocks_of(s):
    return [pl.ds(b * BLOCK, BLOCK) for b in range(s.tokens.shape[0] // BLOCK)]


def project_in(s):
    pairs = s.query.shape[0]
    scale = jnp.asarray((LANES // 2) ** -0.5, BF16)
    for rows in blocks_of(s):
        x = s.tokens[rows, :]
        for weight, target in ((s.w_query, s.query), (s.w_key, s.key), (s.w_value, s.value)):
            y = dot(x, weight[...]).astype(BF16)
            if target is s.query:
                y = y * scale
            for pair in range(pairs):
                target[pair, rows, :] = y[:, pair * LANES : (pair + 1) * LANES]


def attend_in(s):
    position = lax.broadcasted_iota(jnp.int32, (1, s.tokens.shape[0]), 1)
    attend_forward(s, jnp.where(position < s.length, 0.0, -1e30))


def first_norm(s):
    for rows in blocks_of(s):
        out = dot(s.ctx[rows, :], s.w_out[...])
        out_low = out.astype(BF16)
        s.out_low[rows, :] = out_low
        act, slope = gelu_parts(dot(out_low, s.down_one[...], NT))
        act = act.astype(BF16)
        s.act_one[rows, :] = act
        s.slope_one[rows, :] = slope
        hidden = s.tokens[rows, :].astype(F32) + out + dot(act, s.up_one[...])
        unit, inverse = norm_forward(hidden)
        s.unit_one[rows, :] = unit
        s.inverse_one[rows, :] = inverse
        normed = unit * s.gain_one[...] + s.bias_one[...]
        s.normed_low[rows, :] = normed.astype(BF16)
        s.total[rows, :] = jnp.zeros_like(normed)


def feed_forward(s):
    @pl.loop(0, s.w_inner.shape[0])
    def _(tile):
        for rows in blocks_of(s):
            act, slope = gelu_parts(dot(s.normed_low[rows, :], s.w_inner[tile]))
            s.slope[tile, rows, :] = slope.astype(BF16)
            s.total[rows, :] += dot(act.astype(BF16), s.w_outer[tile])


def second_norm(s):
    for rows in blocks_of(s):
        ffn = s.total[rows, :]
        ffn_low = ffn.astype(BF16)
        act, slope = gelu_parts(dot(ffn_low, s.down_two[...], NT))
        act = act.astype(BF16)
        normed = s.unit_one[rows, :] * s.gain_one[...] + s.bias_one[...]
        hidden = normed + ffn + dot(act, s.up_two[...])
        unit, inverse = norm_forward(hidden)
        s.output[rows, :] = (unit * s.gain_two[...] + s.bias_two[...]).astype(BF16)
        dy = s.cotangent[rows, :].astype(F32)
        s.vectors[2:3, :] += jnp.sum(dy * unit, axis=0, keepdims=True)
        s.vectors[3:4, :] += jnp.sum(dy, axis=0, keepdims=True)
        dh = norm_backward(dy, unit, inverse, s.gain_two[...])
        da = dh.astype(BF16)
        s.grads[3, :, :] += dot(act, da, TN)
        dz = (dot(da, s.up_two[...], NT) * slope).astype(BF16)
        s.grads[2, :, :] += dot(dz, ffn_low, TN)
        s.total[rows, :] = dh
        s.dffn[rows, :] = (dh + dot(dz, s.down_two[...])).astype(BF16)


def feed_backward(s):
    @pl.loop(0, s.w_inner.shape[0])
    def _(tile):
        for rows in blocks_of(s):
            du = dot(s.dffn[rows, :], s.w_outer[tile], NT) * s.slope[tile, rows, :].astype(F32)
            s.total[rows, :] += dot(du.astype(BF16), s.w_inner[tile], NT)


def first_norm_backward(s):
    for rows in blocks_of(s):
        dy = s.total[rows, :]
        unit = s.unit_one[rows, :]
        s.vectors[0:1, :] += jnp.sum(dy * unit, axis=0, keepdims=True)
        s.vectors[1:2, :] += jnp.sum(dy, axis=0, keepdims=True)
        dh = norm_backward(dy, unit, s.inverse_one[rows, :], s.gain_one[...])
        s.total[rows, :] = dh
        da = dh.astype(BF16)
        s.grads[1, :, :] += dot(s.act_one[rows, :], da, TN)
        dz = (dot(da, s.up_one[...], NT) * s.slope_one[rows, :]).astype(BF16)
        s.grads[0, :, :] += dot(dz, s.out_low[rows, :], TN)
        dout = (dh + dot(dz, s.down_one[...])).astype(BF16)
        s.ctx[rows, :] = dot(dout, s.w_out[...], NT).astype(BF16)


def project_back(s):
    for rows in blocks_of(s):
        grad = s.total[rows, :] + dot(s.dquery[rows, :], s.w_query[...], NT)
        grad = grad + dot(s.dkey[rows, :], s.w_key[...], NT)
        grad = grad + dot(s.dvalue[rows, :], s.w_value[...], NT)
        s.grad_in[rows, :] = grad.astype(BF16)


PHASES = {
    "project_in": project_in,
    "attend_in": attend_in,
    "first_norm": first_norm,
    "feed_forward": feed_forward,
    "second_norm": second_norm,
    "feed_backward": feed_backward,
    "first_norm_backward": first_norm_backward,
    "attend_backward": attend_backward,
    "project_back": project_back,
}


def small_shapes(width, adapt):
    flat = ((adapt, width), BF16)
    row = ((1, width), F32)
    return dict(zip(INPUTS[6:], (flat,) * 4 + (row,) * 4))


INPUTS = (
    "w_query", "w_key", "w_value", "w_out", "w_inner", "w_outer",
    "down_one", "up_one", "down_two", "up_two",
    "gain_one", "bias_one", "gain_two", "bias_two",
)
BIG = INPUTS[:6]


def layer_scratch(span, width, hidden, adapt):
    pairs, tiles = width // LANES, hidden // width
    v = pltpu.VMEM
    return {
        "v_w_query": v((width, width), BF16),
        "v_w_key": v((width, width), BF16),
        "v_w_value": v((width, width), BF16),
        "v_w_out": v((width, width), BF16),
        "v_w_inner": v((tiles, width, width), BF16),
        "v_w_outer": v((tiles, width, width), BF16),
        "query": v((pairs, span, LANES), BF16),
        "key": v((pairs, span, LANES), BF16),
        "value": v((pairs, span, LANES), BF16),
        "expo": v((2 * pairs, span, span), BF16),
        "inv": v((pairs, span, LANES), F32),
        "attn": v((pairs, span, LANES), F32),
        "ctx": v((span, width), BF16),
        "out_low": v((span, width), BF16),
        "act_one": v((span, adapt), BF16),
        "slope_one": v((span, adapt), F32),
        "unit_one": v((span, width), F32),
        "inverse_one": v((span, 1), F32),
        "normed_low": v((span, width), BF16),
        "slope": v((tiles, span, width), BF16),
        "total": v((span, width), F32),
        "dffn": v((span, width), BF16),
        "dscores": v((2, span, span), BF16),
        "dvalue_t": v((LANES, span), BF16),
        "dkey_t": v((LANES, span), BF16),
        "dquery": v((span, width), BF16),
        "dkey": v((span, width), BF16),
        "dvalue": v((span, width), BF16),
    }


class Reduce:
    def __init__(self, s, parts, devices, me, refs):
        self.s, self.parts, self.me = s, parts, me
        self.outer = devices // GROUP
        self.place = lax.axis_index("dp")
        self.inner = lax.rem(self.place, GROUP)
        self.base = self.place - self.inner
        self.send, self.got_seq, self.part, self.got_dp, self.got_outer, self.full, self.sems = refs

    def seq_peer(self, p):
        return lax.rem(self.me + p, self.parts)

    def inner_peer(self, k):
        return lax.rem(self.inner + k, GROUP)

    def dp_peer(self, k):
        return self.base + self.inner_peer(k)

    def outer_peer(self, k):
        return lax.rem(self.place + k * GROUP, self.outer * GROUP)

    def greeted(self):
        return (
            [{"seq": self.seq_peer(p)} for p in range(1, self.parts)]
            + [{"dp": self.dp_peer(k)} for k in range(1, GROUP)]
            + [{"dp": self.outer_peer(k)} for k in range(1, self.outer)]
        )

    def copy(self, stage, k, source, target, device):
        return pltpu.make_async_remote_copy(
            src_ref=source,
            dst_ref=target,
            send_sem=self.sems.at[0, stage, k],
            recv_sem=self.sems.at[1, stage, k],
            device_id=device,
            device_id_type=MESH,
        )

    def copies(self, stage):
        mine = self.me * GROUP
        if stage == 0:
            return [
                self.copy(
                    0, p, self.send.at[pl.ds(self.seq_peer(p) * GROUP, GROUP)], self.got_seq.at[p], {"seq": self.seq_peer(p)}
                )
                for p in range(1, self.parts)
            ]
        if stage == 1:
            return [
                self.copy(1, k, self.part.at[self.inner_peer(k)], self.got_dp.at[k], {"dp": self.dp_peer(k)})
                for k in range(1, GROUP)
            ]
        if stage == 2:
            return [
                self.copy(2, k, self.got_outer.at[0], self.got_outer.at[k], {"dp": self.outer_peer(k)})
                for k in range(1, self.outer)
            ]
        if stage == 3:
            block = self.full.at[mine + self.inner]
            return [self.copy(3, k, block, block, {"dp": self.dp_peer(k)}) for k in range(1, GROUP)]
        block = self.full.at[pl.ds(mine, GROUP)]
        return [self.copy(4, p, block, block, {"seq": self.seq_peer(p)}) for p in range(1, self.parts)]

    def start(self, stage):
        for copy in self.copies(stage):
            copy.start()

    def finish(self, stage):
        for copy in self.copies(stage):
            copy.wait()

    def first(self):
        grads, vectors = self.s.grads, self.s.vectors
        adapt, width = grads.shape[1:]
        chunks, rows = self.send.shape[:2]
        head = lax.broadcasted_iota(jnp.int32, (rows, LANES), 0) == 0
        pairs = width // LANES
        for c in range(chunks):
            first = c * rows
            self.send[c, :, :width] = grads[first // adapt, first % adapt : first % adapt + rows, :].astype(BF16)
            tail = jnp.zeros((rows, LANES), F32)
            if c < 4 * pairs:
                vector = vectors[c // pairs : c // pairs + 1, (c % pairs) * LANES : (c % pairs + 1) * LANES]
                tail = jnp.where(head, vector, tail)
            self.send[c, :, width:] = tail.astype(BF16)
        self.start(0)

    def second(self):
        self.finish(0)
        total = self.send[pl.ds(self.me * GROUP, GROUP)].astype(F32)
        for p in range(1, self.parts):
            total = total + self.got_seq[p].astype(F32)
        self.part[...] = total.astype(BF16)
        self.start(1)

    def third(self):
        self.finish(1)
        total = self.part[self.inner].astype(F32)
        for k in range(1, GROUP):
            total = total + self.got_dp[k].astype(F32)
        if self.outer > 1:
            self.got_outer[0] = total.astype(BF16)
            self.start(2)
            self.finish(2)
            group = self.place // GROUP
            total = jnp.zeros_like(total)
            for a in range(self.outer):
                total = total + self.got_outer[lax.rem(group + self.outer - a, self.outer)].astype(F32)
        self.full[self.me * GROUP + self.inner] = total.astype(BF16)
        self.start(3)

    def fourth(self):
        self.finish(3)
        self.start(4)

    def last(self, grads, vectors):
        self.finish(4)
        adapt, width = self.s.grads.shape[1:]
        chunks, rows = self.send.shape[:2]
        pairs = width // LANES
        for c in range(chunks):
            first = c * rows
            chunk = self.full[c].astype(F32)
            grads[first // adapt][first % adapt : first % adapt + rows, :] = chunk[:, :width]
            if c < 4 * pairs:
                lanes = slice((c % pairs) * LANES, (c % pairs + 1) * LANES)
                vectors[c // pairs][lanes] = chunk[0, width:]


def layer_kernel(parts, devices, per, lengths, tokens, cotangent, *refs):
    s = Refs()
    refs = list(refs)
    for name in INPUTS:
        setattr(s, name, refs.pop(0))
    for name in INPUTS[10:]:
        setattr(s, name, getattr(s, name)[...].reshape(1, -1))
    hbm = {name: getattr(s, name) for name in BIG}
    output, grad_in = refs.pop(0), refs.pop(0)
    grads_out = [refs.pop(0) for _ in range(4)]
    vectors_out = [refs.pop(0) for _ in range(4)]
    for name in layer_scratch(LANES, LANES, LANES, 8):
        setattr(s, name, refs.pop(0))
    s.grads, s.vectors, x_in, dy_in, out_buf, grad_buf = (refs.pop(0) for _ in range(6))
    w_sem, own_sem, send_sem, recv_sem = (refs.pop(0) for _ in range(4))

    me = lax.axis_index("seq")
    rows = tokens.shape[1]
    mine = pl.ds(me * rows, rows)
    peers = [lax.rem(me + p, parts) for p in range(parts)]
    reduce = Reduce(s, parts, devices, me, refs)

    barrier = pltpu.get_barrier_semaphore()
    for device in reduce.greeted():
        pl.semaphore_signal(barrier, inc=1, device_id=device, device_id_type=MESH)

    width = tokens.shape[2]
    weight_copies = []
    for index, name in enumerate(BIG):
        ref = getattr(s, "v_" + name)
        if name == "w_inner":
            for t in range(ref.shape[0]):
                weight_copies.append(
                    pltpu.make_async_copy(hbm[name].at[:, pl.ds(t * width, width)], ref.at[t], w_sem.at[index, t])
                )
        elif name == "w_outer":
            for t in range(ref.shape[0]):
                weight_copies.append(
                    pltpu.make_async_copy(hbm[name].at[pl.ds(t * width, width), :], ref.at[t], w_sem.at[index, t])
                )
        else:
            weight_copies.append(pltpu.make_async_copy(hbm[name], ref, w_sem.at[index, 0]))
        setattr(s, name, ref)

    pl.semaphore_wait(barrier, len(reduce.greeted()))

    def copies(array, step):
        made = []
        for p in [*range(1, parts), 0]:
            if array < 2:
                source, target = ((tokens, x_in), (cotangent, dy_in))[array]
                source, target = source.at[step * parts + peers[p]], target.at[step, mine]
            else:
                source, target = ((out_buf, output), (grad_buf, grad_in))[array - 2]
                source, target = source.at[step, pl.ds(peers[p] * rows, rows)], target.at[step * parts + me]
            if p == 0:
                made.append(pltpu.make_async_copy(source, target, own_sem.at[array, step]))
            else:
                made.append(
                    pltpu.make_async_remote_copy(
                        src_ref=source,
                        dst_ref=target,
                        send_sem=send_sem.at[array, step, p],
                        recv_sem=recv_sem.at[array, step, p],
                        device_id={"seq": peers[p]},
                        device_id_type=MESH,
                    )
                )
        return made

    def start(array, step):
        for copy in copies(array, step):
            copy.start()

    def finish(array, step):
        for copy in copies(array, step):
            copy.wait()

    start(0, 0)
    for copy in weight_copies:
        copy.start()
    for ref in (s.grads, s.vectors):
        ref[...] = jnp.zeros_like(ref)
    for copy in weight_copies:
        copy.wait()

    @pl.loop(0, per)
    def _(step):
        more, final = step + 1 < per, step == per - 1
        s.tokens, s.cotangent = x_in.at[step], dy_in.at[step]
        s.output, s.grad_in = out_buf.at[step], grad_buf.at[step]
        s.length = lengths[step * parts + me]
        finish(0, step)

        @pl.when(step == 0)
        def _():
            start(1, 0)

        @pl.when(more)
        def _():
            start(0, step + 1)

        project_in(s)
        attend_in(s)
        first_norm(s)
        feed_forward(s)
        finish(1, step)

        @pl.when(more)
        def _():
            start(1, step + 1)

        second_norm(s)
        start(2, step)
        feed_backward(s)
        first_norm_backward(s)

        @pl.when(final)
        def _():
            reduce.first()

        def hook(pair):
            for at, stage in ((1, reduce.second), (3, reduce.third), (5, reduce.fourth)):
                pl.when(final & (pair == at))(stage)

        attend_backward(s, hook)
        project_back(s)
        start(3, step)

    reduce.last(grads_out, vectors_out)

    @pl.loop(0, per)
    def _(step):
        finish(2, step)
        finish(3, step)


def per_device(parts, devices, tokens, lengths, cotangent, *params):
    batch, rows, width = tokens.shape
    hidden, adapt = params[4].shape[1], params[6].shape[1]
    per, span = batch // parts, parts * rows
    chunks, chunk_rows = parts * GROUP, 4 * adapt // (parts * GROUP)
    outer = devices // GROUP
    params = list(params)
    params[6], params[8] = params[6].T, params[8].T
    vmem = pl.BlockSpec(memory_space=pltpu.VMEM)
    anywhere = pl.BlockSpec(memory_space=pl.ANY)
    dma = pltpu.SemaphoreType.DMA
    scratch = [
        *layer_scratch(span, width, hidden, adapt).values(),
        pltpu.VMEM((4, adapt, width), F32),
        pltpu.VMEM((8, width), F32),
        *[pltpu.VMEM((per, span, width), BF16)] * 4,
        dma((len(BIG), hidden // width)),
        dma((4, per)),
        dma((4, per, parts)),
        dma((4, per, parts)),
    ]
    chunk = (chunk_rows, width + LANES)
    scratch += [
        pltpu.VMEM((chunks, *chunk), BF16),
        pltpu.VMEM((parts, GROUP, *chunk), BF16),
        pltpu.VMEM((GROUP, *chunk), BF16),
        pltpu.VMEM((GROUP, *chunk), BF16),
        pltpu.VMEM((outer, *chunk), BF16),
        pltpu.VMEM((chunks, *chunk), BF16),
        dma((2, 5, max(parts, GROUP, outer))),
    ]
    results = pl.pallas_call(
        functools.partial(layer_kernel, parts, devices, per),
        out_shape=(jax.ShapeDtypeStruct((batch, rows, width), BF16),) * 2
        + (jax.ShapeDtypeStruct((adapt, width), F32),) * 4
        + (jax.ShapeDtypeStruct((width,), F32),) * 4,
        in_specs=[pl.BlockSpec(memory_space=pltpu.SMEM)]
        + [anywhere] * 2
        + [anywhere if name in BIG else vmem for name in INPUTS],
        out_specs=(anywhere,) * 2 + (vmem,) * 8,
        scratch_shapes=scratch,
        compiler_params=pltpu.CompilerParams(
            collective_id=0, has_side_effects=True, vmem_limit_bytes=62 * 2**20
        ),
        name="layer",
    )(lengths, tokens, cotangent, *params)
    output, grad_in, down_one, up_one, down_two, up_two, *vectors = results
    return (output, grad_in.astype(F32), down_one.T, up_one, down_two.T, up_two, *vectors)


def solution(mesh):
    split = P("dp", "seq", None)
    return jax.shard_map(
        functools.partial(per_device, mesh.shape["seq"], mesh.shape["dp"]),
        mesh=mesh,
        in_specs=(split, P("dp"), split) + (P(),) * 14,
        out_specs=(split, split) + (P(),) * 8,
        check_vma=False,
    )
```

time: 333 us -> 175 us (0.53)
  waiting for transfers between devices: 87.7 us -> 0 us
  blocking collectives: 38.8 us -> 0 us
  between operations: 14.1 us -> 0.72 us
  local copies, waits for them, and re-layouts: 17.4 us -> 6.53 us
  Pallas kernels: 170 us -> 163 us
    psum x1 -> x0, waiting for transfers between devices: 87.6 us -> none  [per_device(): lax.psum((grads[0], grads[1], grads[2], grads[3], vectors), ('dp', 'seq'))]
    psum x1 -> x0, blocking collectives: 38.8 us -> none  [per_device(): lax.psum((grads[0], grads[1], grads[2], grads[3], vectors), ('dp', 'seq'))]
    pallas_call x1, Pallas kernels: 170 us -> 163 us  [per_device(): pl.pallas_call(functools.partial(layer_kernel, parts, devices, per), out_...]
    reshape x4 -> x0, local copies, waits for them, and re-layouts: 5.07 us -> none  [per_device(): params = [p.reshape(1, width) if p.ndim == 1 else p for p in params]]
    unnamed x19 -> x27, local copies, waits for them, and re-layouts: 9.44 us -> 6.53 us
  transfers between devices with their start and end apart: 1 -> 0, of which waited for: 1 -> 0; matrix products, arithmetic and copies ran while one was open for 1% -> 0% of each run, Pallas kernels for 0% -> 0%
where the time goes in v2:
time: 175 us
  Pallas kernels  163 us (93%)
  local copies, waits for them, and re-layouts  6.53 us (4%)
  other arithmetic  4.47 us (3%)
    pallas_call x1, Pallas kernels, per_device(): pl.pallas_call(functools.partial(layer_kernel, parts, devices, per), out_...  163 us
    unnamed x27, local copies, waits for them, and re-layouts  6.53 us
    convert_element_type x1, other arithmetic, per_device(): grad_in.astype(F32)  4.47 us

profile of v2, /device:TPU:1, one launch (start us, length us, event | category | flops | bytes accessed | tf_op | source)
XLA Modules:
  0.0 174.9 jit_solution(14736400028227564181)
XLA Ops:
  0.7 163.2 %layer.1 = (bf16[12,128,768]{2,1,0:T(8,128)(2,1)}, bf16[12,128,768]{2,1,0:T(8,128)(2,1)}, f32[64,768]{1,0:T(8,128)}, f32[64,768]{1,0:T(8,128)}, f32[64,768]{1,0:...) custom-call(s32[12]{0:T(128)} %lengths.1, ...), custom_call_target="tpu_custom_call" | custom-call | tf_op jit(solution)/shard_map/layer/pallas_call | solution.py:589
  163.8 0.0 copy-start
  163.8 4.5 %convert_element_type.3 = f32[12,128,768]{2,1,0:T(8,128)} convert(bf16[12,128,768]{2,1,0:T(8,128)(2,1)} %get-tuple-element.21) | non-fusion elementwise | flops 1179648 | bytes 7077888 | tf_op jit(solution)/shard_map/convert_element_type | solution.py:605
  168.3 0.0 copy-done
  168.3 0.0 copy-start.4
  168.3 0.0 copy-start.3
  168.3 0.0 copy-start.2
  168.3 0.0 copy-start.1
  168.3 0.0 copy-start.8
  168.3 0.0 copy-start.7
  168.3 0.0 copy-start.6
  168.4 0.0 copy-start.5
  168.4 1.4 copy.36
  169.8 0.0 copy-done.4
  169.8 0.7 copy.37
  170.5 0.0 copy-done.3
  170.5 0.7 copy.38
  171.1 0.0 copy-done.2
  171.1 0.7 copy.39
  171.8 0.0 copy-done.1
  171.8 0.7 copy.40
  172.5 0.0 copy-done.8
  172.5 0.6 copy.41
  173.1 0.0 copy-done.7
  173.1 0.6 copy.42
  173.7 0.0 copy-done.6
  173.7 0.6 copy.43
  174.3 0.0 copy-done.5
  174.3 0.6 copy.44
Async XLA Ops:
  163.8 4.5 %copy-start = (bf16[12,128,768]{2,1,0:T(8,128)(2,1)S(1)}, bf16[12,128,768]{2,1,0:T(8,128)(2,1)}, u32[]{:S(2)}) copy-start(bf16[12,128,768]{2,1,0:T(8,128)(2,1)} %get-tuple-element.40) | copy-start | bytes 7077892
  168.3 1.5 copy-start.4
  168.3 2.1 %copy-start.3 = (f32[64,768]{1,0:T(8,128)S(1)}, f32[64,768]{1,0:T(8,128)}, u32[]{:S(2)}) copy-start(f32[64,768]{1,0:T(8,128)} %get-tuple-element.43) | copy-start | bytes 589828
  168.3 2.8 %copy-start.2 = (f32[64,768]{1,0:T(8,128)S(1)}, f32[64,768]{1,0:T(8,128)}, u32[]{:S(2)}) copy-start(f32[64,768]{1,0:T(8,128)} %get-tuple-element.24) | copy-start | bytes 589828
  168.3 3.5 %copy-start.1 = (f32[64,768]{1,0:T(8,128)S(1)}, f32[64,768]{1,0:T(8,128)}, u32[]{:S(2)}) copy-start(f32[64,768]{1,0:T(8,128)} %get-tuple-element.45) | copy-start | bytes 589828
  168.3 4.2 %copy-start.8 = (f32[768]{0:T(1024)S(1)}, f32[768]{0:T(1024)}, u32[]{:S(2)}) copy-start(f32[768]{0:T(1024)} %get-tuple-element.46) | copy-start | bytes 9220
  168.3 4.8 %copy-start.7 = (f32[768]{0:T(1024)S(1)}, f32[768]{0:T(1024)}, u32[]{:S(2)}) copy-start(f32[768]{0:T(1024)} %get-tuple-element.47) | copy-start | bytes 9220
  168.3 5.3 %copy-start.6 = (f32[768]{0:T(1024)S(1)}, f32[768]{0:T(1024)}, u32[]{:S(2)}) copy-start(f32[768]{0:T(1024)} %get-tuple-element.48) | copy-start | bytes 9220
  168.4 5.9 %copy-start.5 = (f32[768]{0:T(1024)S(1)}, f32[768]{0:T(1024)}, u32[]{:S(2)}) copy-start(f32[768]{0:T(1024)} %get-tuple-element.49) | copy-start | bytes 9220

commit v3 on v2

--- a/solution.py
+++ b/solution.py
@@ -49,76 +49,59 @@
     pass
 
 
-def attend_forward(s, bias):
-    span = s.query.shape[1]
-    half = span // 2
+def pair_lanes(pair):
+    return slice(pair * LANES, (pair + 1) * LANES)
+
+
+def attend_forward(s):
+    pairs, span = s.query.shape[:2]
     low = lax.broadcasted_iota(jnp.int32, (1, LANES), 1) < LANES // 2
-
-    @pl.loop(0, s.query.shape[0])
-    def _(pair):
+    bias = jnp.where(lax.broadcasted_iota(jnp.int32, (1, span), 1) < s.length, 0.0, -1e30)
+    for pair in range(pairs):
         key, value = s.key[pair], s.value[pair]
         zero = jnp.zeros_like(key)
         keys = (jnp.where(low, key, zero), jnp.where(low, zero, key))
-        for block in range(2):
-            rows = pl.ds(block * half, half)
+        value = jnp.concatenate([value, jnp.ones_like(value)], axis=1)
+        for rows in blocks_of(s):
             query = s.query[pair, rows, :]
-            outs, invs = [], []
+            outs, totals = [], []
             for head in range(2):
                 scores = dot(query, keys[head], NT) + bias
-                top = jnp.max(scores, axis=-1, keepdims=True)
-                expo = jnp.exp(scores - top)
-                total = jnp.sum(expo, axis=-1, keepdims=True)
-                expo_low = expo.astype(BF16)
-                s.expo[2 * pair + head, rows, :] = expo_low
-                outs.append(dot(expo_low, value))
-                invs.append(1.0 / total)
-            inv = jnp.where(low, invs[0], invs[1])
-            attn = jnp.where(low, outs[0], outs[1]) * inv
+                expo = jnp.exp(scores - jnp.max(scores, axis=-1, keepdims=True)).astype(BF16)
+                s.expo[2 * pair + head, rows, :] = expo
+                product = dot(expo, value)
+                outs.append(product[:, :LANES])
+                totals.append(product[:, LANES:])
+            inv = 1.0 / jnp.where(low, *totals)
+            attn = jnp.where(low, *outs) * inv
             s.inv[pair, rows, :] = inv
             s.attn[pair, rows, :] = attn
-            s.ctx[rows, pl.ds(pl.multiple_of(pair * LANES, LANES), LANES)] = attn.astype(BF16)
-
-
-def attend_backward(s, hook=None):
-    span = s.query.shape[1]
-    half = span // 2
+            s.ctx[rows, pair_lanes(pair)] = attn.astype(BF16)
+
+
+def attend_backward(s, pair):
     low = lax.broadcasted_iota(jnp.int32, (1, LANES), 1) < LANES // 2
-
-    @pl.loop(0, s.query.shape[0])
-    def _(pair):
-        if hook is not None:
-            hook(pair)
-        lanes = pl.ds(pl.multiple_of(pair * LANES, LANES), LANES)
-        key, value, query = s.key[pair], s.value[pair], s.query[pair]
-        zero = jnp.zeros_like(key)
-        keys = (jnp.where(low, key, zero), jnp.where(low, zero, key))
-        wide = s.ctx[:, lanes].astype(F32) * s.inv[pair]
-        terms = wide * s.attn[pair]
-        deltas = (
-            jnp.sum(jnp.where(low, terms, 0.0), axis=-1, keepdims=True),
-            jnp.sum(jnp.where(low, 0.0, terms), axis=-1, keepdims=True),
-        )
-        grad = wide.astype(BF16)
-        grads = (jnp.where(low, grad, zero), jnp.where(low, zero, grad))
-        grad_t, query_t = grad.T, query.T
-        dquery = [None, None]
-        for head in range(2):
-            sub = slice(head * LANES // 2, (head + 1) * LANES // 2)
-            for block in range(2):
-                rows = slice(block * half, (block + 1) * half)
-                expo = s.expo[2 * pair + head, pl.ds(block * half, half), :]
-                dprob = dot(grads[head][rows], value, NT)
-                dscores = (expo.astype(F32) * (dprob - deltas[head][rows])).astype(BF16)
-                s.dscores[head, pl.ds(block * half, half), :] = dscores
-                part = dot(dscores, keys[head])
-                dquery[block] = part if head == 0 else dquery[block] + part
-            s.dvalue_t[sub, :] = dot(grad_t[sub], s.expo[2 * pair + head]).astype(BF16)
-            s.dkey_t[sub, :] = dot(query_t[sub], s.dscores[head]).astype(BF16)
-        scale = (LANES // 2) ** -0.5
-        for block in range(2):
-            s.dquery[pl.ds(block * half, half), lanes] = (dquery[block] * scale).astype(BF16)
-        s.dkey[:, lanes] = s.dkey_t[...].T
-        s.dvalue[:, lanes] = s.dvalue_t[...].T
+    lanes = pair_lanes(pair)
+    key, value, query = s.key[pair], s.value[pair], s.query[pair]
+    zero = jnp.zeros_like(key)
+    wide = s.ctx[:, lanes].astype(F32) * s.inv[pair]
+    terms = wide * s.attn[pair]
+    grad = wide.astype(BF16)
+    grad_t, query_t = grad.T, query.T
+    dquery, dkey, dvalue = 0.0, [], []
+    for head in range(2):
+        mine = low if head == 0 else ~low
+        sub = slice(head * LANES // 2, (head + 1) * LANES // 2)
+        delta = jnp.sum(jnp.where(mine, terms, 0.0), axis=-1, keepdims=True)
+        expo = s.expo[2 * pair + head]
+        dprob = dot(jnp.where(mine, grad, zero), value, NT)
+        dscores = (expo.astype(F32) * (dprob - delta)).astype(BF16)
+        dquery = dquery + dot(dscores, jnp.where(mine, key, zero))
+        dvalue.append(dot(grad_t[sub], expo).astype(BF16))
+        dkey.append(dot(query_t[sub], dscores).astype(BF16))
+    s.dquery[:, lanes] = (dquery * (LANES // 2) ** -0.5).astype(BF16)
+    s.dkey[:, lanes] = jnp.concatenate(dkey, axis=0).T
+    s.dvalue[:, lanes] = jnp.concatenate(dvalue, axis=0).T
 
 
 BLOCK = 256
@@ -139,11 +122,6 @@
                 y = y * scale
             for pair in range(pairs):
                 target[pair, rows, :] = y[:, pair * LANES : (pair + 1) * LANES]
-
-
-def attend_in(s):
-    position = lax.broadcasted_iota(jnp.int32, (1, s.tokens.shape[0]), 1)
-    attend_forward(s, jnp.where(position < s.length, 0.0, -1e30))
 
 
 def first_norm(s):
@@ -165,8 +143,7 @@
 
 
 def feed_forward(s):
-    @pl.loop(0, s.w_inner.shape[0])
-    def _(tile):
+    for tile in range(s.w_inner.shape[0]):
         for rows in blocks_of(s):
             act, slope = gelu_parts(dot(s.normed_low[rows, :], s.w_inner[tile]))
             s.slope[tile, rows, :] = slope.astype(BF16)
@@ -196,8 +173,7 @@
 
 
 def feed_backward(s):
-    @pl.loop(0, s.w_inner.shape[0])
-    def _(tile):
+    for tile in range(s.w_inner.shape[0]):
         for rows in blocks_of(s):
             du = dot(s.dffn[rows, :], s.w_outer[tile], NT) * s.slope[tile, rows, :].astype(F32)
             s.total[rows, :] += dot(du.astype(BF16), s.w_inner[tile], NT)
@@ -229,13 +205,13 @@
 
 PHASES = {
     "project_in": project_in,
-    "attend_in": attend_in,
+    "attend_forward": attend_forward,
     "first_norm": first_norm,
     "feed_forward": feed_forward,
     "second_norm": second_norm,
     "feed_backward": feed_backward,
     "first_norm_backward": first_norm_backward,
-    "attend_backward": attend_backward,
+    "attend_backward": lambda s: [attend_backward(s, pair) for pair in range(6)],
     "project_back": project_back,
 }
 
@@ -280,9 +256,6 @@
         "slope": v((tiles, span, width), BF16),
         "total": v((span, width), F32),
         "dffn": v((span, width), BF16),
-        "dscores": v((2, span, span), BF16),
-        "dvalue_t": v((LANES, span), BF16),
-        "dkey_t": v((LANES, span), BF16),
         "dquery": v((span, width), BF16),
         "dkey": v((span, width), BF16),
         "dvalue": v((span, width), BF16),
@@ -521,7 +494,7 @@
             start(0, step + 1)
 
         project_in(s)
-        attend_in(s)
+        attend_forward(s)
         first_norm(s)
         feed_forward(s)
         finish(1, step)
@@ -539,11 +512,11 @@
         def _():
             reduce.first()
 
-        def hook(pair):
-            for at, stage in ((1, reduce.second), (3, reduce.third), (5, reduce.fourth)):
-                pl.when(final & (pair == at))(stage)
-
-        attend_backward(s, hook)
+        stages = {1: reduce.second, 3: reduce.third, 5: reduce.fourth}
+        for pair in range(s.query.shape[0]):
+            attend_backward(s, pair)
+            if pair in stages:
+                pl.when(final)(stages[pair])
         project_back(s)
         start(3, step)
 

time: 175 us -> 151 us (0.86)
  Pallas kernels: 163 us -> 139 us
    pallas_call x1, Pallas kernels: 163 us -> 139 us  [per_device(): pl.pallas_call(functools.partial(layer_kernel, parts, devices, per), out_...]
where the time goes in v3:
time: 151 us
  Pallas kernels  139 us (92%)
  local copies, waits for them, and re-layouts  6.53 us (4%)
  other arithmetic  4.47 us (3%)
    pallas_call x1, Pallas kernels, per_device(): pl.pallas_call(functools.partial(layer_kernel, parts, devices, per), out_...  139 us
    unnamed x27, local copies, waits for them, and re-layouts  6.53 us
    convert_element_type x1, other arithmetic, per_device(): grad_in.astype(F32)  4.47 us

profile of v3, /device:TPU:1, one launch (start us, length us, event | category | flops | bytes accessed | tf_op | source)
XLA Modules:
  0.0 150.7 jit_solution(11530246440615295440)
XLA Ops:
  0.7 138.9 %layer.1 = (bf16[12,128,768]{2,1,0:T(8,128)(2,1)}, bf16[12,128,768]{2,1,0:T(8,128)(2,1)}, f32[64,768]{1,0:T(8,128)}, f32[64,768]{1,0:T(8,128)}, f32[64,768]{1,0:...) custom-call(s32[12]{0:T(128)} %lengths.1, ...), custom_call_target="tpu_custom_call" | custom-call | tf_op jit(solution)/shard_map/layer/pallas_call | solution.py:562
  139.6 0.0 copy-start
  139.6 4.5 %convert_element_type.3 = f32[12,128,768]{2,1,0:T(8,128)} convert(bf16[12,128,768]{2,1,0:T(8,128)(2,1)} %get-tuple-element.21) | non-fusion elementwise | flops 1179648 | bytes 7077888 | tf_op jit(solution)/shard_map/convert_element_type | solution.py:578
  144.1 0.0 copy-done
  144.1 0.0 copy-start.4
  144.1 0.0 copy-start.3
  144.1 0.0 copy-start.2
  144.1 0.0 copy-start.1
  144.1 0.0 copy-start.8
  144.1 0.0 copy-start.7
  144.1 0.0 copy-start.6
  144.1 0.0 copy-start.5
  144.1 1.4 copy.36
  145.6 0.0 copy-done.4
  145.6 0.7 copy.37
  146.2 0.0 copy-done.3
  146.2 0.7 copy.38
  146.9 0.0 copy-done.2
  146.9 0.7 copy.39
  147.6 0.0 copy-done.1
  147.6 0.7 copy.40
  148.3 0.0 copy-done.8
  148.3 0.6 copy.41
  148.9 0.0 copy-done.7
  148.9 0.6 copy.42
  149.5 0.0 copy-done.6
  149.5 0.6 copy.43
  150.1 0.0 copy-done.5
  150.1 0.6 copy.44
Async XLA Ops:
  139.6 4.5 %copy-start = (bf16[12,128,768]{2,1,0:T(8,128)(2,1)S(1)}, bf16[12,128,768]{2,1,0:T(8,128)(2,1)}, u32[]{:S(2)}) copy-start(bf16[12,128,768]{2,1,0:T(8,128)(2,1)} %get-tuple-element.40) | copy-start | bytes 7077892
  144.1 1.5 copy-start.4
  144.1 2.1 %copy-start.3 = (f32[64,768]{1,0:T(8,128)S(1)}, f32[64,768]{1,0:T(8,128)}, u32[]{:S(2)}) copy-start(f32[64,768]{1,0:T(8,128)} %get-tuple-element.43) | copy-start | bytes 589828
  144.1 2.8 %copy-start.2 = (f32[64,768]{1,0:T(8,128)S(1)}, f32[64,768]{1,0:T(8,128)}, u32[]{:S(2)}) copy-start(f32[64,768]{1,0:T(8,128)} %get-tuple-element.24) | copy-start | bytes 589828
  144.1 3.5 %copy-start.1 = (f32[64,768]{1,0:T(8,128)S(1)}, f32[64,768]{1,0:T(8,128)}, u32[]{:S(2)}) copy-start(f32[64,768]{1,0:T(8,128)} %get-tuple-element.45) | copy-start | bytes 589828
  144.1 4.2 %copy-start.8 = (f32[768]{0:T(1024)S(1)}, f32[768]{0:T(1024)}, u32[]{:S(2)}) copy-start(f32[768]{0:T(1024)} %get-tuple-element.46) | copy-start | bytes 9220
  144.1 4.8 %copy-start.7 = (f32[768]{0:T(1024)S(1)}, f32[768]{0:T(1024)}, u32[]{:S(2)}) copy-start(f32[768]{0:T(1024)} %get-tuple-element.47) | copy-start | bytes 9220
  144.1 5.3 %copy-start.6 = (f32[768]{0:T(1024)S(1)}, f32[768]{0:T(1024)}, u32[]{:S(2)}) copy-start(f32[768]{0:T(1024)} %get-tuple-element.48) | copy-start | bytes 9220
  144.1 5.9 %copy-start.5 = (f32[768]{0:T(1024)S(1)}, f32[768]{0:T(1024)}, u32[]{:S(2)}) copy-start(f32[768]{0:T(1024)} %get-tuple-element.49) | copy-start | bytes 9220

commit v4 on v3

--- a/solution.py
+++ b/solution.py
@@ -107,8 +107,8 @@
 BLOCK = 256
 
 
-def blocks_of(s):
-    return [pl.ds(b * BLOCK, BLOCK) for b in range(s.tokens.shape[0] // BLOCK)]
+def blocks_of(s, block=BLOCK):
+    return [pl.ds(b * block, block) for b in range(s.tokens.shape[0] // block)]
 
 
 def project_in(s):
@@ -125,7 +125,7 @@
 
 
 def first_norm(s):
-    for rows in blocks_of(s):
+    for rows in blocks_of(s, 512):
         out = dot(s.ctx[rows, :], s.w_out[...])
         out_low = out.astype(BF16)
         s.out_low[rows, :] = out_low
@@ -150,8 +150,22 @@
             s.total[rows, :] += dot(act.astype(BF16), s.w_outer[tile])
 
 
+def vector_slots(width):
+    pairs = width // LANES
+    per = pl.cdiv(2 * pairs, 2 * GROUP)
+    return [
+        (2 * side + i // pairs, i % pairs, side, i // per, i % per) for side in range(2) for i in range(2 * pairs)
+    ]
+
+
+def add_vector(s, which, value):
+    for vector, piece, side, chunk, row in vector_slots(value.shape[-1]):
+        if vector == which:
+            s.vectors[side, chunk, row : row + 1, :] += value[:, pair_lanes(piece)]
+
+
 def second_norm(s):
-    for rows in blocks_of(s):
+    for rows in blocks_of(s, 512):
         ffn = s.total[rows, :]
         ffn_low = ffn.astype(BF16)
         act, slope = gelu_parts(dot(ffn_low, s.down_two[...], NT))
@@ -161,8 +175,8 @@
         unit, inverse = norm_forward(hidden)
         s.output[rows, :] = (unit * s.gain_two[...] + s.bias_two[...]).astype(BF16)
         dy = s.cotangent[rows, :].astype(F32)
-        s.vectors[2:3, :] += jnp.sum(dy * unit, axis=0, keepdims=True)
-        s.vectors[3:4, :] += jnp.sum(dy, axis=0, keepdims=True)
+        add_vector(s, 2, jnp.sum(dy * unit, axis=0, keepdims=True))
+        add_vector(s, 3, jnp.sum(dy, axis=0, keepdims=True))
         dh = norm_backward(dy, unit, inverse, s.gain_two[...])
         da = dh.astype(BF16)
         s.grads[3, :, :] += dot(act, da, TN)
@@ -183,8 +197,8 @@
     for rows in blocks_of(s):
         dy = s.total[rows, :]
         unit = s.unit_one[rows, :]
-        s.vectors[0:1, :] += jnp.sum(dy * unit, axis=0, keepdims=True)
-        s.vectors[1:2, :] += jnp.sum(dy, axis=0, keepdims=True)
+        add_vector(s, 0, jnp.sum(dy * unit, axis=0, keepdims=True))
+        add_vector(s, 1, jnp.sum(dy, axis=0, keepdims=True))
         dh = norm_backward(dy, unit, s.inverse_one[rows, :], s.gain_one[...])
         s.total[rows, :] = dh
         da = dh.astype(BF16)
@@ -263,67 +277,55 @@
 
 
 class Reduce:
-    def __init__(self, s, parts, devices, me, refs):
-        self.s, self.parts, self.me = s, parts, me
-        self.outer = devices // GROUP
-        self.place = lax.axis_index("dp")
-        self.inner = lax.rem(self.place, GROUP)
-        self.base = self.place - self.inner
-        self.send, self.got_seq, self.part, self.got_dp, self.got_outer, self.full, self.sems = refs
-
-    def seq_peer(self, p):
-        return lax.rem(self.me + p, self.parts)
-
-    def inner_peer(self, k):
-        return lax.rem(self.inner + k, GROUP)
-
-    def dp_peer(self, k):
-        return self.base + self.inner_peer(k)
-
-    def outer_peer(self, k):
-        return lax.rem(self.place + k * GROUP, self.outer * GROUP)
+    def __init__(self, s, side, parts, devices, me, refs):
+        self.s, self.side = s, side
+        self.half, self.pair = lax.rem(me, 2), me // 2
+        self.pairs, self.outer = parts // 2, devices // GROUP
+        place = lax.axis_index("dp")
+        self.inner, self.group = lax.rem(place, GROUP), place // GROUP
+        self.send, self.got_near, self.part, self.got_dp, self.got_far, self.full, self.sems = (
+            ref.at[side] for ref in refs
+        )
+        self.near = {"seq": me + 1 - 2 * self.half}
+        self.ring = [lax.rem(self.inner + k, GROUP) for k in range(GROUP)]
+        self.across = [{"dp": self.group * GROUP + k} for k in self.ring]
+        self.far = [
+            {
+                "seq": lax.rem(self.pair + k % self.pairs, self.pairs) * 2 + self.half,
+                "dp": lax.rem(self.group + k // self.pairs, self.outer) * GROUP + self.inner,
+            }
+            for k in range(self.pairs * self.outer)
+        ]
 
     def greeted(self):
-        return (
-            [{"seq": self.seq_peer(p)} for p in range(1, self.parts)]
-            + [{"dp": self.dp_peer(k)} for k in range(1, GROUP)]
-            + [{"dp": self.outer_peer(k)} for k in range(1, self.outer)]
-        )
-
-    def copy(self, stage, k, source, target, device):
-        return pltpu.make_async_remote_copy(
-            src_ref=source,
-            dst_ref=target,
-            send_sem=self.sems.at[0, stage, k],
-            recv_sem=self.sems.at[1, stage, k],
-            device_id=device,
-            device_id_type=MESH,
-        )
+        return [self.near, *self.across[1:], *self.far[1:]]
 
     def copies(self, stage):
-        mine = self.me * GROUP
+        mine, theirs = self.half * GROUP, (1 - self.half) * GROUP
         if stage == 0:
-            return [
-                self.copy(
-                    0, p, self.send.at[pl.ds(self.seq_peer(p) * GROUP, GROUP)], self.got_seq.at[p], {"seq": self.seq_peer(p)}
-                )
-                for p in range(1, self.parts)
-            ]
-        if stage == 1:
-            return [
-                self.copy(1, k, self.part.at[self.inner_peer(k)], self.got_dp.at[k], {"dp": self.dp_peer(k)})
-                for k in range(1, GROUP)
-            ]
-        if stage == 2:
-            return [
-                self.copy(2, k, self.got_outer.at[0], self.got_outer.at[k], {"dp": self.outer_peer(k)})
-                for k in range(1, self.outer)
-            ]
-        if stage == 3:
+            moves = [(self.send.at[pl.ds(theirs, GROUP)], self.got_near, self.near)]
+        elif stage == 1:
+            moves = [(self.part.at[self.ring[k]], self.got_dp.at[k], self.across[k]) for k in range(1, GROUP)]
+        elif stage == 2:
+            block = self.got_far.at[self.group * self.pairs + self.pair]
+            moves = [(block, block, device) for device in self.far[1:]]
+        elif stage == 3:
             block = self.full.at[mine + self.inner]
-            return [self.copy(3, k, block, block, {"dp": self.dp_peer(k)}) for k in range(1, GROUP)]
-        block = self.full.at[pl.ds(mine, GROUP)]
-        return [self.copy(4, p, block, block, {"seq": self.seq_peer(p)}) for p in range(1, self.parts)]
+            moves = [(block, block, device) for device in self.across[1:]]
+        else:
+            block = self.full.at[pl.ds(mine, GROUP)]
+            moves = [(block, block, self.near)]
+        return [
+            pltpu.make_async_remote_copy(
+                src_ref=source,
+                dst_ref=target,
+                send_sem=self.sems.at[0, stage, k],
+                recv_sem=self.sems.at[1, stage, k],
+                device_id=device,
+                device_id_type=MESH,
+            )
+            for k, (source, target, device) in enumerate(moves)
+        ]
 
     def start(self, stage):
         for copy in self.copies(stage):
@@ -337,23 +339,16 @@
         grads, vectors = self.s.grads, self.s.vectors
         adapt, width = grads.shape[1:]
         chunks, rows = self.send.shape[:2]
-        head = lax.broadcasted_iota(jnp.int32, (rows, LANES), 0) == 0
-        pairs = width // LANES
         for c in range(chunks):
-            first = c * rows
-            self.send[c, :, :width] = grads[first // adapt, first % adapt : first % adapt + rows, :].astype(BF16)
-            tail = jnp.zeros((rows, LANES), F32)
-            if c < 4 * pairs:
-                vector = vectors[c // pairs : c // pairs + 1, (c % pairs) * LANES : (c % pairs + 1) * LANES]
-                tail = jnp.where(head, vector, tail)
-            self.send[c, :, width:] = tail.astype(BF16)
+            at = c * rows
+            matrix = 2 * self.side + at // adapt
+            self.send[c, :, :width] = grads[matrix, at % adapt : at % adapt + rows, :].astype(BF16)
+            self.send[c, :, width:] = vectors[self.side, c].astype(BF16)
         self.start(0)
 
     def second(self):
         self.finish(0)
-        total = self.send[pl.ds(self.me * GROUP, GROUP)].astype(F32)
-        for p in range(1, self.parts):
-            total = total + self.got_seq[p].astype(F32)
+        total = self.send[pl.ds(self.half * GROUP, GROUP)].astype(F32) + self.got_near[...].astype(F32)
         self.part[...] = total.astype(BF16)
         self.start(1)
 
@@ -362,33 +357,20 @@
         total = self.part[self.inner].astype(F32)
         for k in range(1, GROUP):
             total = total + self.got_dp[k].astype(F32)
-        if self.outer > 1:
-            self.got_outer[0] = total.astype(BF16)
-            self.start(2)
-            self.finish(2)
-            group = self.place // GROUP
-            total = jnp.zeros_like(total)
-            for a in range(self.outer):
-                total = total + self.got_outer[lax.rem(group + self.outer - a, self.outer)].astype(F32)
-        self.full[self.me * GROUP + self.inner] = total.astype(BF16)
+        self.got_far[self.group * self.pairs + self.pair] = total.astype(BF16)
+        self.start(2)
+
+    def fourth(self):
+        self.finish(2)
+        total = self.got_far[0].astype(F32)
+        for k in range(1, self.pairs * self.outer):
+            total = total + self.got_far[k].astype(F32)
+        self.full[self.half * GROUP + self.inner] = total.astype(BF16)
         self.start(3)
 
-    def fourth(self):
+    def fifth(self):
         self.finish(3)
         self.start(4)
-
-    def last(self, grads, vectors):
-        self.finish(4)
-        adapt, width = self.s.grads.shape[1:]
-        chunks, rows = self.send.shape[:2]
-        pairs = width // LANES
-        for c in range(chunks):
-            first = c * rows
-            chunk = self.full[c].astype(F32)
-            grads[first // adapt][first % adapt : first % adapt + rows, :] = chunk[:, :width]
-            if c < 4 * pairs:
-                lanes = slice((c % pairs) * LANES, (c % pairs + 1) * LANES)
-                vectors[c // pairs][lanes] = chunk[0, width:]
 
 
 def layer_kernel(parts, devices, per, lengths, tokens, cotangent, *refs):
@@ -399,9 +381,7 @@
     for name in INPUTS[10:]:
         setattr(s, name, getattr(s, name)[...].reshape(1, -1))
     hbm = {name: getattr(s, name) for name in BIG}
-    output, grad_in = refs.pop(0), refs.pop(0)
-    grads_out = [refs.pop(0) for _ in range(4)]
-    vectors_out = [refs.pop(0) for _ in range(4)]
+    output, grad_in, full = (refs.pop(0) for _ in range(3))
     for name in layer_scratch(LANES, LANES, LANES, 8):
         setattr(s, name, refs.pop(0))
     s.grads, s.vectors, x_in, dy_in, out_buf, grad_buf = (refs.pop(0) for _ in range(6))
@@ -410,11 +390,16 @@
     me = lax.axis_index("seq")
     rows = tokens.shape[1]
     mine = pl.ds(me * rows, rows)
-    peers = [lax.rem(me + p, parts) for p in range(parts)]
-    reduce = Reduce(s, parts, devices, me, refs)
+    near = me + 1 - 2 * lax.rem(me, 2)
+    peers = [near] + [
+        lax.rem(me // 2 + k, parts // 2) * 2 + core for core in range(2) for k in range(1, parts // 2)
+    ]
+    refs.insert(5, full)
+    one, two = (Reduce(s, side, parts, devices, me, refs) for side in range(2))
 
     barrier = pltpu.get_barrier_semaphore()
-    for device in reduce.greeted():
+    greeted = [{"seq": peer} for peer in peers] + one.greeted()
+    for device in greeted:
         pl.semaphore_signal(barrier, inc=1, device_id=device, device_id_type=MESH)
 
     width = tokens.shape[2]
@@ -435,39 +420,35 @@
             weight_copies.append(pltpu.make_async_copy(hbm[name], ref, w_sem.at[index, 0]))
         setattr(s, name, ref)
 
-    pl.semaphore_wait(barrier, len(reduce.greeted()))
-
-    def copies(array, step):
-        made = []
-        for p in [*range(1, parts), 0]:
-            if array < 2:
-                source, target = ((tokens, x_in), (cotangent, dy_in))[array]
-                source, target = source.at[step * parts + peers[p]], target.at[step, mine]
-            else:
-                source, target = ((out_buf, output), (grad_buf, grad_in))[array - 2]
-                source, target = source.at[step, pl.ds(peers[p] * rows, rows)], target.at[step * parts + me]
-            if p == 0:
-                made.append(pltpu.make_async_copy(source, target, own_sem.at[array, step]))
-            else:
-                made.append(
-                    pltpu.make_async_remote_copy(
-                        src_ref=source,
-                        dst_ref=target,
-                        send_sem=send_sem.at[array, step, p],
-                        recv_sem=recv_sem.at[array, step, p],
-                        device_id={"seq": peers[p]},
-                        device_id_type=MESH,
-                    )
-                )
-        return made
+    pl.semaphore_wait(barrier, len(greeted))
+
+    def move(array, step, peer, slot):
+        if array < 2:
+            source, target = ((tokens, x_in), (cotangent, dy_in))[array]
+            source, target = source.at[step * parts + peer], target.at[step, mine]
+        else:
+            source, target = ((out_buf, output), (grad_buf, grad_in))[array - 2]
+            source, target = source.at[step, pl.ds(peer * rows, rows)], target.at[step * parts + me]
+        if slot is None:
+            return pltpu.make_async_copy(source, target, own_sem.at[array, step])
+        return pltpu.make_async_remote_copy(
+            src_ref=source,
+            dst_ref=target,
+            send_sem=send_sem.at[array, step, peer],
+            recv_sem=recv_sem.at[array, step, slot],
+            device_id={"seq": peer},
+            device_id_type=MESH,
+        )
 
     def start(array, step):
-        for copy in copies(array, step):
-            copy.start()
+        for peer in peers:
+            move(array, step, peer, me).start()
+        move(array, step, me, None).start()
 
     def finish(array, step):
-        for copy in copies(array, step):
-            copy.wait()
+        for peer in peers:
+            move(array, step, peer, peer).wait()
+        move(array, step, me, None).wait()
 
     start(0, 0)
     for copy in weight_copies:
@@ -503,24 +484,40 @@
         def _():
             start(1, step + 1)
 
+        at_end = pl.when(final)
         second_norm(s)
         start(2, step)
+
+        @at_end
+        def _():
+            two.first()
+            two.second()
+
         feed_backward(s)
         first_norm_backward(s)
 
-        @pl.when(final)
+        @at_end
         def _():
-            reduce.first()
-
-        stages = {1: reduce.second, 3: reduce.third, 5: reduce.fourth}
+            one.first()
+            two.third()
+            one.second()
+
         for pair in range(s.query.shape[0]):
             attend_backward(s, pair)
-            if pair in stages:
-                pl.when(final)(stages[pair])
+
+        @at_end
+        def _():
+            one.third()
+            two.fourth()
+
         project_back(s)
         start(3, step)
 
-    reduce.last(grads_out, vectors_out)
+    one.fourth()
+    two.fifth()
+    one.fifth()
+    one.finish(4)
+    two.finish(4)
 
     @pl.loop(0, per)
     def _(step):
@@ -528,54 +525,82 @@
         finish(3, step)
 
 
+def tail_kernel(output, grad_in, full, output_out, grad_in_out, *grads):
+    output_out[...] = output[...]
+    grad_in_out[...] = grad_in[...].astype(F32)
+
+    @pl.when(pl.program_id(0) == 0)
+    def _():
+        matrices, vectors = grads[:4], grads[4:]
+        adapt, width = matrices[0].shape
+        chunks, rows = full.shape[1:3]
+        for side in range(2):
+            for c in range(chunks):
+                at = c * rows
+                matrix = matrices[2 * side + at // adapt]
+                matrix[at % adapt : at % adapt + rows, :] = full[side, c, :, :width].astype(F32)
+        tails = full[:, :, :, width:].astype(F32)
+        for vector, piece, side, chunk, row in vector_slots(width):
+            vectors[vector][pair_lanes(piece)] = tails[side, chunk, row]
+
+
 def per_device(parts, devices, tokens, lengths, cotangent, *params):
     batch, rows, width = tokens.shape
     hidden, adapt = params[4].shape[1], params[6].shape[1]
     per, span = batch // parts, parts * rows
-    chunks, chunk_rows = parts * GROUP, 4 * adapt // (parts * GROUP)
-    outer = devices // GROUP
+    chunks, chunk_rows = 2 * GROUP, adapt // GROUP
+    far = parts // 2 * (devices // GROUP)
     params = list(params)
     params[6], params[8] = params[6].T, params[8].T
     vmem = pl.BlockSpec(memory_space=pltpu.VMEM)
     anywhere = pl.BlockSpec(memory_space=pl.ANY)
     dma = pltpu.SemaphoreType.DMA
+    chunk = (chunk_rows, width + LANES)
     scratch = [
         *layer_scratch(span, width, hidden, adapt).values(),
         pltpu.VMEM((4, adapt, width), F32),
-        pltpu.VMEM((8, width), F32),
+        pltpu.VMEM((2, chunks, chunk_rows, LANES), F32),
         *[pltpu.VMEM((per, span, width), BF16)] * 4,
         dma((len(BIG), hidden // width)),
         dma((4, per)),
         dma((4, per, parts)),
         dma((4, per, parts)),
+        pltpu.VMEM((2, chunks, *chunk), BF16),
+        *[pltpu.VMEM((2, GROUP, *chunk), BF16)] * 3,
+        pltpu.VMEM((2, far, *chunk), BF16),
+        dma((2, 2, 5, max(GROUP, far))),
     ]
-    chunk = (chunk_rows, width + LANES)
-    scratch += [
-        pltpu.VMEM((chunks, *chunk), BF16),
-        pltpu.VMEM((parts, GROUP, *chunk), BF16),
-        pltpu.VMEM((GROUP, *chunk), BF16),
-        pltpu.VMEM((GROUP, *chunk), BF16),
-        pltpu.VMEM((outer, *chunk), BF16),
-        pltpu.VMEM((chunks, *chunk), BF16),
-        dma((2, 5, max(parts, GROUP, outer))),
-    ]
-    results = pl.pallas_call(
+    moved = jax.ShapeDtypeStruct((batch, rows, width), BF16)
+    summed = jax.ShapeDtypeStruct((2, chunks, *chunk), BF16)
+    output, grad_in, full = pl.pallas_call(
         functools.partial(layer_kernel, parts, devices, per),
-        out_shape=(jax.ShapeDtypeStruct((batch, rows, width), BF16),) * 2
-        + (jax.ShapeDtypeStruct((adapt, width), F32),) * 4
-        + (jax.ShapeDtypeStruct((width,), F32),) * 4,
+        out_shape=(moved, moved, summed),
         in_specs=[pl.BlockSpec(memory_space=pltpu.SMEM)]
         + [anywhere] * 2
         + [anywhere if name in BIG else vmem for name in INPUTS],
-        out_specs=(anywhere,) * 2 + (vmem,) * 8,
+        out_specs=(anywhere, anywhere, vmem),
         scratch_shapes=scratch,
         compiler_params=pltpu.CompilerParams(
             collective_id=0, has_side_effects=True, vmem_limit_bytes=62 * 2**20
         ),
         name="layer",
     )(lengths, tokens, cotangent, *params)
-    output, grad_in, down_one, up_one, down_two, up_two, *vectors = results
-    return (output, grad_in.astype(F32), down_one.T, up_one, down_two.T, up_two, *vectors)
+    block = pl.BlockSpec((batch // 2, rows, width), lambda i: (i, 0, 0))
+    whole = [pl.BlockSpec((adapt, width), lambda i: (0, 0))] * 4 + [pl.BlockSpec((width,), lambda i: (0,))] * 4
+    output, grad_in, down_one, up_one, down_two, up_two, *vectors = pl.pallas_call(
+        tail_kernel,
+        grid=(2,),
+        out_shape=(
+            moved,
+            jax.ShapeDtypeStruct((batch, rows, width), F32),
+            *[jax.ShapeDtypeStruct((adapt, width), F32)] * 4,
+            *[jax.ShapeDtypeStruct((width,), F32)] * 4,
+        ),
+        in_specs=[block, block, pl.BlockSpec(summed.shape, lambda i: (0, 0, 0, 0))],
+        out_specs=(block, block, *whole),
+        name="tail",
+    )(output, grad_in, full)
+    return (output, grad_in, down_one.T, up_one, down_two.T, up_two, *vectors)
 
 
 def solution(mesh):

time: 151 us -> 133 us (0.88)
  Pallas kernels: 139 us -> 132 us
  local copies, waits for them, and re-layouts: 6.53 us -> 0 us
  other arithmetic: 4.47 us -> 0 us
    pallas_call x1, Pallas kernels: 139 us -> 127 us  [per_device(): pl.pallas_call(functools.partial(layer_kernel, parts, devices, per), out_...]
    unnamed x27 -> x0, local copies, waits for them, and re-layouts: 6.53 us -> none
    pallas_call x0 -> x1, Pallas kernels: none -> 5.19 us  [per_device(): pl.pallas_call(tail_kernel, grid=(2,), out_shape=(moved, jax.ShapeDtypeSt...]
    convert_element_type x1 -> x0, other arithmetic: 4.47 us -> none  [per_device(): grad_in.astype(F32)]
where the time goes in v4:
time: 133 us
  Pallas kernels  132 us (99%)
    pallas_call x1, Pallas kernels, per_device(): pl.pallas_call(functools.partial(layer_kernel, parts, devices, per), out_...  127 us
    pallas_call x1, Pallas kernels, per_device(): pl.pallas_call(tail_kernel, grid=(2,), out_shape=(moved, jax.ShapeDtypeSt...  5.19 us

profile of v4, /device:TPU:1, one launch (start us, length us, event | category | flops | bytes accessed | tf_op | source)
XLA Modules:
  0.0 132.6 jit_solution(4182727574159543138)
XLA Ops:
  0.6 126.8 %layer.1 = (bf16[12,128,768]{2,1,0:T(8,128)(2,1)}, bf16[12,128,768]{2,1,0:T(8,128)(2,1)}, bf16[2,16,8,896]{3,2,1,0:T(8,128)(2,1)}) custom-call(s32[12]{0:T(128)} %lengths.1, bf16[12,128,768]{2,1,0:T(8,128)(2,1)} %tokens.1, bf16[12,128,768]{2,1,0:T(8,128)(2,1)} %cotangent.1, bf16[768,768]{1,0:T(8,128)(2,1)} %refs_0_.1, bf16[768,768]{1,0:T(8,128)(2,1)} %refs_1_.1, ...), custom_call_target="tpu_custom_call" | custom-call | tf_op jit(solution)/shard_map/layer/pallas_call | solution.py:575
  127.4 5.2 %tail.1 = (bf16[12,128,768]{2,1,0:T(8,128)(2,1)}, f32[12,128,768]{2,1,0:T(8,128)}, f32[64,768]{1,0:T(8,128)}, f32[64,768]{1,0:T(8,128)}, f32[64,768]{1,0:T(8,128...) custom-call(bf16[12,128,768]{2,1,0:T(8,128)(2,1)} %get-tuple-element.23.output, ...), custom_call_target="tpu_custom_call" | custom-call | tf_op jit(solution)/shard_map/tail/pallas_call | solution.py:590

commit v5 on v4

--- a/solution.py
+++ b/solution.py
@@ -56,7 +56,11 @@
 def attend_forward(s):
     pairs, span = s.query.shape[:2]
     low = lax.broadcasted_iota(jnp.int32, (1, LANES), 1) < LANES // 2
-    bias = jnp.where(lax.broadcasted_iota(jnp.int32, (1, span), 1) < s.length, 0.0, -1e30)
+    column = lax.broadcasted_iota(jnp.int32, (1, span), 1)
+    position = column
+    for at, shift in s.shifts:
+        position = jnp.where(column >= at, column + shift, position)
+    bias = jnp.where(position < s.length, 0.0, -1e30)
     for pair in range(pairs):
         key, value = s.key[pair], s.value[pair]
         zero = jnp.zeros_like(key)
@@ -99,9 +103,14 @@
         dquery = dquery + dot(dscores, jnp.where(mine, key, zero))
         dvalue.append(dot(grad_t[sub], expo).astype(BF16))
         dkey.append(dot(query_t[sub], dscores).astype(BF16))
-    s.dquery[:, lanes] = (dquery * (LANES // 2) ** -0.5).astype(BF16)
-    s.dkey[:, lanes] = jnp.concatenate(dkey, axis=0).T
-    s.dvalue[:, lanes] = jnp.concatenate(dvalue, axis=0).T
+    grads = (
+        (dquery * (LANES // 2) ** -0.5).astype(BF16),
+        jnp.concatenate(dkey, axis=0).T,
+        jnp.concatenate(dvalue, axis=0).T,
+    )
+    for which, grad in enumerate(grads):
+        s.near_grads[which, :, lanes] = grad[: s.near_rows]
+        s.far_grads[which, :, lanes] = grad[s.near_rows :]
 
 
 BLOCK = 256
@@ -111,10 +120,15 @@
     return [pl.ds(b * block, block) for b in range(s.tokens.shape[0] // block)]
 
 
-def project_in(s):
+def far_blocks(s):
+    near, span = s.near_rows, s.tokens.shape[0]
+    return [pl.ds(at, BLOCK) for at in range(near, span, BLOCK)]
+
+
+def project_in(s, blocks):
     pairs = s.query.shape[0]
     scale = jnp.asarray((LANES // 2) ** -0.5, BF16)
-    for rows in blocks_of(s):
+    for rows in blocks:
         x = s.tokens[rows, :]
         for weight, target in ((s.w_query, s.query), (s.w_key, s.key), (s.w_value, s.value)):
             y = dot(x, weight[...]).astype(BF16)
@@ -173,8 +187,8 @@
         normed = s.unit_one[rows, :] * s.gain_one[...] + s.bias_one[...]
         hidden = normed + ffn + dot(act, s.up_two[...])
         unit, inverse = norm_forward(hidden)
+        dy = s.cotangent[rows, :].astype(F32)
         s.output[rows, :] = (unit * s.gain_two[...] + s.bias_two[...]).astype(BF16)
-        dy = s.cotangent[rows, :].astype(F32)
         add_vector(s, 2, jnp.sum(dy * unit, axis=0, keepdims=True))
         add_vector(s, 3, jnp.sum(dy, axis=0, keepdims=True))
         dh = norm_backward(dy, unit, inverse, s.gain_two[...])
@@ -194,13 +208,16 @@
 
 
 def first_norm_backward(s):
-    for rows in blocks_of(s):
+    for rows in [pl.ds(0, s.near_rows), *far_blocks(s)]:
         dy = s.total[rows, :]
         unit = s.unit_one[rows, :]
         add_vector(s, 0, jnp.sum(dy * unit, axis=0, keepdims=True))
         add_vector(s, 1, jnp.sum(dy, axis=0, keepdims=True))
         dh = norm_backward(dy, unit, s.inverse_one[rows, :], s.gain_one[...])
-        s.total[rows, :] = dh
+        if rows.start == 0:
+            s.near_total[...] = dh
+        else:
+            s.total[rows, :] = dh
         da = dh.astype(BF16)
         s.grads[1, :, :] += dot(s.act_one[rows, :], da, TN)
         dz = (dot(da, s.up_one[...], NT) * s.slope_one[rows, :]).astype(BF16)
@@ -209,31 +226,14 @@
         s.ctx[rows, :] = dot(dout, s.w_out[...], NT).astype(BF16)
 
 
-def project_back(s):
-    for rows in blocks_of(s):
-        grad = s.total[rows, :] + dot(s.dquery[rows, :], s.w_query[...], NT)
-        grad = grad + dot(s.dkey[rows, :], s.w_key[...], NT)
-        grad = grad + dot(s.dvalue[rows, :], s.w_value[...], NT)
-        s.grad_in[rows, :] = grad.astype(BF16)
-
-
-PHASES = {
-    "project_in": project_in,
-    "attend_forward": attend_forward,
-    "first_norm": first_norm,
-    "feed_forward": feed_forward,
-    "second_norm": second_norm,
-    "feed_backward": feed_backward,
-    "first_norm_backward": first_norm_backward,
-    "attend_backward": lambda s: [attend_backward(s, pair) for pair in range(6)],
-    "project_back": project_back,
-}
-
-
-def small_shapes(width, adapt):
-    flat = ((adapt, width), BF16)
-    row = ((1, width), F32)
-    return dict(zip(INPUTS[6:], (flat,) * 4 + (row,) * 4))
+def project_back(s, total, grads, target):
+    weights = (s.w_query, s.w_key, s.w_value)
+    rows = target.shape[0]
+    for block in [pl.ds(at, min(BLOCK, rows)) for at in range(0, rows, BLOCK)]:
+        grad = total[block, :]
+        for which, weight in enumerate(weights):
+            grad = grad + dot(grads[which, block, :], weight[...], NT)
+        target[block, :] = grad.astype(BF16)
 
 
 INPUTS = (
@@ -244,7 +244,7 @@
 BIG = INPUTS[:6]
 
 
-def layer_scratch(span, width, hidden, adapt):
+def layer_scratch(span, near, per, width, hidden, adapt):
     pairs, tiles = width // LANES, hidden // width
     v = pltpu.VMEM
     return {
@@ -254,9 +254,9 @@
         "v_w_out": v((width, width), BF16),
         "v_w_inner": v((tiles, width, width), BF16),
         "v_w_outer": v((tiles, width, width), BF16),
-        "query": v((pairs, span, LANES), BF16),
-        "key": v((pairs, span, LANES), BF16),
-        "value": v((pairs, span, LANES), BF16),
+        "all_query": v((per, pairs, span, LANES), BF16),
+        "all_key": v((per, pairs, span, LANES), BF16),
+        "all_value": v((per, pairs, span, LANES), BF16),
         "expo": v((2 * pairs, span, span), BF16),
         "inv": v((pairs, span, LANES), F32),
         "attn": v((pairs, span, LANES), F32),
@@ -270,9 +270,9 @@
         "slope": v((tiles, span, width), BF16),
         "total": v((span, width), F32),
         "dffn": v((span, width), BF16),
-        "dquery": v((span, width), BF16),
-        "dkey": v((span, width), BF16),
-        "dvalue": v((span, width), BF16),
+        "all_near_grads": v((per, 3, near, width), BF16),
+        "all_near_total": v((per, near, width), F32),
+        "far_grads": v((3, span - near, width), BF16),
     }
 
 
@@ -382,23 +382,31 @@
         setattr(s, name, getattr(s, name)[...].reshape(1, -1))
     hbm = {name: getattr(s, name) for name in BIG}
     output, grad_in, full = (refs.pop(0) for _ in range(3))
-    for name in layer_scratch(LANES, LANES, LANES, 8):
+    for name in layer_scratch(LANES, 8, 1, LANES, LANES, 8):
         setattr(s, name, refs.pop(0))
-    s.grads, s.vectors, x_in, dy_in, out_buf, grad_buf = (refs.pop(0) for _ in range(6))
+    s.grads, s.vectors, x_in, dy_in = (refs.pop(0) for _ in range(4))
     w_sem, own_sem, send_sem, recv_sem = (refs.pop(0) for _ in range(4))
 
     me = lax.axis_index("seq")
     rows = tokens.shape[1]
-    mine = pl.ds(me * rows, rows)
-    near = me + 1 - 2 * lax.rem(me, 2)
-    peers = [near] + [
-        lax.rem(me // 2 + k, parts // 2) * 2 + core for core in range(2) for k in range(1, parts // 2)
-    ]
+    couples = parts // 2
+    core, couple = lax.rem(me, 2), me // 2
+    s.near_rows = 2 * rows
+    s.shifts = []
+    for k in range(couples):
+        s.shifts.append((k * 2 * rows, (lax.rem(couple + k, couples) - k) * 2 * rows))
+    near = [(0, 1 - core)]
+    far = [(k, c) for c in range(2) for k in range(1, couples)]
+
+    def index_of(peer):
+        k, c = peer
+        return lax.rem(couple + k, couples) * 2 + c
+
     refs.insert(5, full)
     one, two = (Reduce(s, side, parts, devices, me, refs) for side in range(2))
 
     barrier = pltpu.get_barrier_semaphore()
-    greeted = [{"seq": peer} for peer in peers] + one.greeted()
+    greeted = [{"seq": index_of(peer)} for peer in near + far] + one.greeted()
     for device in greeted:
         pl.semaphore_signal(barrier, inc=1, device_id=device, device_id_type=MESH)
 
@@ -423,70 +431,91 @@
     pl.semaphore_wait(barrier, len(greeted))
 
     def move(array, step, peer, slot):
+        k, c = (0, core) if peer is None else peer
+        other = me if peer is None else index_of(peer)
+        outside, inside = ((tokens, x_in), (cotangent, dy_in), (output, dy_in), (grad_in, x_in))[array]
         if array < 2:
-            source, target = ((tokens, x_in), (cotangent, dy_in))[array]
-            source, target = source.at[step * parts + peer], target.at[step, mine]
+            source = outside.at[step * parts + other]
+            target = inside.at[step, pl.ds((couples - k) % couples * 2 * rows + core * rows, rows)]
         else:
-            source, target = ((out_buf, output), (grad_buf, grad_in))[array - 2]
-            source, target = source.at[step, pl.ds(peer * rows, rows)], target.at[step * parts + me]
-        if slot is None:
+            source = inside.at[step, pl.ds(k * 2 * rows + c * rows, rows)]
+            target = outside.at[step * parts + me]
+        if peer is None:
             return pltpu.make_async_copy(source, target, own_sem.at[array, step])
         return pltpu.make_async_remote_copy(
             src_ref=source,
             dst_ref=target,
-            send_sem=send_sem.at[array, step, peer],
-            recv_sem=recv_sem.at[array, step, slot],
-            device_id={"seq": peer},
+            send_sem=send_sem.at[array, step, other],
+            recv_sem=recv_sem.at[array, step, other if slot is None else slot],
+            device_id={"seq": other},
             device_id_type=MESH,
         )
 
-    def start(array, step):
+    def start(array, step, peers):
         for peer in peers:
             move(array, step, peer, me).start()
-        move(array, step, me, None).start()
-
-    def finish(array, step):
+
+    def finish(array, step, peers):
         for peer in peers:
-            move(array, step, peer, peer).wait()
-        move(array, step, me, None).wait()
-
-    start(0, 0)
+            move(array, step, peer, None).wait()
+
+    near = near + [None]
+    everyone = far + near
+
+    def view(step):
+        s.tokens, s.cotangent = x_in.at[step], dy_in.at[step]
+        s.query, s.key, s.value = (ref.at[step] for ref in (s.all_query, s.all_key, s.all_value))
+        s.near_grads, s.near_total = s.all_near_grads.at[step], s.all_near_total.at[step]
+        s.output = s.cotangent
+        s.length = lengths[step * parts + me]
+
+    near_rows, far_rows = pl.ds(0, s.near_rows), pl.ds(s.near_rows, x_in.shape[1] - s.near_rows)
+    start(0, 0, far)
+    for step in range(per):
+        start(0, step, near)
     for copy in weight_copies:
         copy.start()
     for ref in (s.grads, s.vectors):
         ref[...] = jnp.zeros_like(ref)
-    for copy in weight_copies:
+    for copy in weight_copies[:3]:
+        copy.wait()
+
+    @pl.loop(0, per)
+    def _(step):
+        view(step)
+        finish(0, step, near)
+        project_in(s, [near_rows])
+
+    for copy in weight_copies[3:]:
         copy.wait()
 
     @pl.loop(0, per)
     def _(step):
         more, final = step + 1 < per, step == per - 1
-        s.tokens, s.cotangent = x_in.at[step], dy_in.at[step]
-        s.output, s.grad_in = out_buf.at[step], grad_buf.at[step]
-        s.length = lengths[step * parts + me]
-        finish(0, step)
+        view(step)
+        finish(0, step, far)
 
         @pl.when(step == 0)
         def _():
-            start(1, 0)
+            start(1, 0, everyone)
 
         @pl.when(more)
         def _():
-            start(0, step + 1)
-
-        project_in(s)
+            start(0, step + 1, far)
+
+        project_in(s, far_blocks(s))
         attend_forward(s)
         first_norm(s)
         feed_forward(s)
-        finish(1, step)
+        finish(1, step, everyone)
 
         @pl.when(more)
         def _():
-            start(1, step + 1)
+            start(1, step + 1, everyone)
 
         at_end = pl.when(final)
         second_norm(s)
-        start(2, step)
+        start(2, step, everyone)
 
         @at_end
         def _():
@@ -510,19 +539,24 @@
             one.third()
             two.fourth()
 
-        project_back(s)
-        start(3, step)
-
-    one.fourth()
-    two.fifth()
+        project_back(s, s.total.at[far_rows], s.far_grads, x_in.at[step, far_rows])
+        start(3, step, far)
+
+    for step in range(per):
+        view(step)
+        project_back(s, s.near_total, s.near_grads, x_in.at[step, near_rows])
+        start(3, step, near)
+        if step == min(1, per - 1):
+            one.fourth()
+            two.fifth()
     one.fifth()
     one.finish(4)
     two.finish(4)
 
     @pl.loop(0, per)
     def _(step):
-        finish(2, step)
-        finish(3, step)
+        finish(2, step, everyone)
+        finish(3, step, everyone)
 
 
 def tail_kernel(output, grad_in, full, output_out, grad_in_out, *grads):
@@ -557,10 +591,10 @@
     dma = pltpu.SemaphoreType.DMA
     chunk = (chunk_rows, width + LANES)
     scratch = [
-        *layer_scratch(span, width, hidden, adapt).values(),
+        *layer_scratch(span, 2 * rows, per, width, hidden, adapt).values(),
         pltpu.VMEM((4, adapt, width), F32),
         pltpu.VMEM((2, chunks, chunk_rows, LANES), F32),
-        *[pltpu.VMEM((per, span, width), BF16)] * 4,
+        *[pltpu.VMEM((per, span, width), BF16)] * 2,
         dma((len(BIG), hidden // width)),
         dma((4, per)),
         dma((4, per, parts)),

time: 133 us -> 129 us (0.970)
  Pallas kernels: 132 us -> 128 us
    pallas_call x1, Pallas kernels: 127 us -> 123 us  [per_device(): pl.pallas_call(functools.partial(layer_kernel, parts, devices, per), out_...]
where the time goes in v5:
time: 129 us
  Pallas kernels  128 us (99%)
    pallas_call x1, Pallas kernels, per_device(): pl.pallas_call(functools.partial(layer_kernel, parts, devices, per), out_...  123 us
    pallas_call x1, Pallas kernels, per_device(): pl.pallas_call(tail_kernel, grid=(2,), out_shape=(moved, jax.ShapeDtypeSt...  5.19 us

profile of v5, /device:TPU:1, one launch (start us, length us, event | category | flops | bytes accessed | tf_op | source)
XLA Modules:
  0.0 128.7 jit_solution(1487892859507547330)
XLA Ops:
  0.6 122.7 %layer.1 = (bf16[12,128,768]{2,1,0:T(8,128)(2,1)}, bf16[12,128,768]{2,1,0:T(8,128)(2,1)}, bf16[2,16,8,896]{3,2,1,0:T(8,128)(2,1)}) custom-call(s32[12]{0:T(128)} %lengths.1, bf16[12,128,768]{2,1,0:T(8,128)(2,1)} %tokens.1, bf16[12,128,768]{2,1,0:T(8,128)(2,1)} %cotangent.1, bf16[768,768]{1,0:T(8,128)(2,1)} %refs_0_.1, bf16[768,768]{1,0:T(8,128)(2,1)} %refs_1_.1, ...), custom_call_target="tpu_custom_call" | custom-call | tf_op jit(solution)/shard_map/layer/pallas_call | solution.py:609
  123.4 5.2 %tail.1 = (bf16[12,128,768]{2,1,0:T(8,128)(2,1)}, f32[12,128,768]{2,1,0:T(8,128)}, f32[64,768]{1,0:T(8,128)}, f32[64,768]{1,0:T(8,128)}, f32[64,768]{1,0:T(8,128...) custom-call(bf16[12,128,768]{2,1,0:T(8,128)(2,1)} %get-tuple-element.23.output, ...), custom_call_target="tpu_custom_call" | custom-call | tf_op jit(solution)/shard_map/tail/pallas_call | solution.py:624

commit v6 on v5

--- a/solution.py
+++ b/solution.py
@@ -516,28 +516,23 @@
         at_end = pl.when(final)
         second_norm(s)
         start(2, step, everyone)
+        feed_backward(s)
+        first_norm_backward(s)
 
         @at_end
         def _():
             two.first()
+            one.first()
             two.second()
-
-        feed_backward(s)
-        first_norm_backward(s)
+            one.second()
+
+        for pair in range(s.query.shape[0]):
+            attend_backward(s, pair)
 
         @at_end
         def _():
-            one.first()
             two.third()
-            one.second()
-
-        for pair in range(s.query.shape[0]):
-            attend_backward(s, pair)
-
-        @at_end
-        def _():
             one.third()
-            two.fourth()
 
         project_back(s, s.total.at[far_rows], s.far_grads, x_in.at[step, far_rows])
         start(3, step, far)
@@ -546,9 +541,10 @@
         view(step)
         project_back(s, s.near_total, s.near_grads, x_in.at[step, near_rows])
         start(3, step, near)
-        if step == min(1, per - 1):
+        if step == 0:
+            two.fourth()
             one.fourth()
-            two.fifth()
+    two.fifth()
     one.fifth()
     one.finish(4)
     two.finish(4)

time: 129 us -> 127 us (0.984)
  Pallas kernels: 128 us -> 126 us
    pallas_call x1, Pallas kernels: 123 us -> 121 us  [per_device(): pl.pallas_call(functools.partial(layer_kernel, parts, devices, per), out_...]
where the time goes in v6:
time: 127 us
  Pallas kernels  126 us (99%)
    pallas_call x1, Pallas kernels, per_device(): pl.pallas_call(functools.partial(layer_kernel, parts, devices, per), out_...  121 us
    pallas_call x1, Pallas kernels, per_device(): pl.pallas_call(tail_kernel, grid=(2,), out_shape=(moved, jax.ShapeDtypeSt...  5.19 us

profile of v6, /device:TPU:1, one launch (start us, length us, event | category | flops | bytes accessed | tf_op | source)
XLA Modules:
  0.0 126.8 jit_solution(6813698392095089144)
XLA Ops:
  0.6 120.8 %layer.1 = (bf16[12,128,768]{2,1,0:T(8,128)(2,1)}, bf16[12,128,768]{2,1,0:T(8,128)(2,1)}, bf16[2,16,8,896]{3,2,1,0:T(8,128)(2,1)}) custom-call(s32[12]{0:T(128)} %lengths.1, bf16[12,128,768]{2,1,0:T(8,128)(2,1)} %tokens.1, bf16[12,128,768]{2,1,0:T(8,128)(2,1)} %cotangent.1, bf16[768,768]{1,0:T(8,128)(2,1)} %refs_0_.1, bf16[768,768]{1,0:T(8,128)(2,1)} %refs_1_.1, ...), custom_call_target="tpu_custom_call" | custom-call | tf_op jit(solution)/shard_map/layer/pallas_call | solution.py:605
  121.5 5.2 %tail.1 = (bf16[12,128,768]{2,1,0:T(8,128)(2,1)}, f32[12,128,768]{2,1,0:T(8,128)}, f32[64,768]{1,0:T(8,128)}, f32[64,768]{1,0:T(8,128)}, f32[64,768]{1,0:T(8,128...) custom-call(bf16[12,128,768]{2,1,0:T(8,128)(2,1)} %get-tuple-element.23.output, ...), custom_call_target="tpu_custom_call" | custom-call | tf_op jit(solution)/shard_map/tail/pallas_call | solution.py:620

commit v7 on v6

--- a/solution.py
+++ b/solution.py
@@ -178,26 +178,41 @@
             s.vectors[side, chunk, row : row + 1, :] += value[:, pair_lanes(piece)]
 
 
-def second_norm(s):
-    for rows in blocks_of(s, 512):
-        ffn = s.total[rows, :]
-        ffn_low = ffn.astype(BF16)
-        act, slope = gelu_parts(dot(ffn_low, s.down_two[...], NT))
-        act = act.astype(BF16)
-        normed = s.unit_one[rows, :] * s.gain_one[...] + s.bias_one[...]
-        hidden = normed + ffn + dot(act, s.up_two[...])
-        unit, inverse = norm_forward(hidden)
-        dy = s.cotangent[rows, :].astype(F32)
-        s.output[rows, :] = (unit * s.gain_two[...] + s.bias_two[...]).astype(BF16)
-        add_vector(s, 2, jnp.sum(dy * unit, axis=0, keepdims=True))
-        add_vector(s, 3, jnp.sum(dy, axis=0, keepdims=True))
-        dh = norm_backward(dy, unit, inverse, s.gain_two[...])
-        da = dh.astype(BF16)
-        s.grads[3, :, :] += dot(act, da, TN)
-        dz = (dot(da, s.up_two[...], NT) * slope).astype(BF16)
-        s.grads[2, :, :] += dot(dz, ffn_low, TN)
-        s.total[rows, :] = dh
-        s.dffn[rows, :] = (dh + dot(dz, s.down_two[...])).astype(BF16)
+def lockstep(stages):
+    stages = list(stages)
+    while stages:
+        for stage in list(stages):
+            try:
+                next(stage)
+            except StopIteration:
+                stages.remove(stage)
+
+
+def second_norm(s, rows):
+    ffn = s.total[rows, :]
+    ffn_low = ffn.astype(BF16)
+    zed = dot(ffn_low, s.down_two[...], NT)
+    yield
+    act, slope = gelu_parts(zed)
+    act = act.astype(BF16)
+    branch = dot(act, s.up_two[...])
+    yield
+    normed = s.unit_one[rows, :] * s.gain_one[...] + s.bias_one[...]
+    unit, inverse = norm_forward(normed + ffn + branch)
+    dy = s.cotangent[rows, :].astype(F32)
+    s.output[rows, :] = (unit * s.gain_two[...] + s.bias_two[...]).astype(BF16)
+    add_vector(s, 2, jnp.sum(dy * unit, axis=0, keepdims=True))
+    add_vector(s, 3, jnp.sum(dy, axis=0, keepdims=True))
+    dh = norm_backward(dy, unit, inverse, s.gain_two[...])
+    s.total[rows, :] = dh
+    da = dh.astype(BF16)
+    yield
+    back = dot(da, s.up_two[...], NT)
+    s.grads[3, :, :] += dot(act, da, TN)
+    yield
+    dz = (back * slope).astype(BF16)
+    s.dffn[rows, :] = (dh + dot(dz, s.down_two[...])).astype(BF16)
+    s.grads[2, :, :] += dot(dz, ffn_low, TN)
 
 
 def feed_backward(s):
@@ -207,23 +222,27 @@
             s.total[rows, :] += dot(du.astype(BF16), s.w_inner[tile], NT)
 
 
-def first_norm_backward(s):
-    for rows in [pl.ds(0, s.near_rows), *far_blocks(s)]:
-        dy = s.total[rows, :]
-        unit = s.unit_one[rows, :]
-        add_vector(s, 0, jnp.sum(dy * unit, axis=0, keepdims=True))
-        add_vector(s, 1, jnp.sum(dy, axis=0, keepdims=True))
-        dh = norm_backward(dy, unit, s.inverse_one[rows, :], s.gain_one[...])
-        if rows.start == 0:
-            s.near_total[...] = dh
-        else:
-            s.total[rows, :] = dh
-        da = dh.astype(BF16)
-        s.grads[1, :, :] += dot(s.act_one[rows, :], da, TN)
-        dz = (dot(da, s.up_one[...], NT) * s.slope_one[rows, :]).astype(BF16)
-        s.grads[0, :, :] += dot(dz, s.out_low[rows, :], TN)
-        dout = (dh + dot(dz, s.down_one[...])).astype(BF16)
-        s.ctx[rows, :] = dot(dout, s.w_out[...], NT).astype(BF16)
+def first_norm_backward(s, rows):
+    dy = s.total[rows, :]
+    unit = s.unit_one[rows, :]
+    add_vector(s, 0, jnp.sum(dy * unit, axis=0, keepdims=True))
+    add_vector(s, 1, jnp.sum(dy, axis=0, keepdims=True))
+    dh = norm_backward(dy, unit, s.inverse_one[rows, :], s.gain_one[...])
+    if rows.start == 0:
+        s.near_total[...] = dh
+    else:
+        s.total[rows, :] = dh
+    da = dh.astype(BF16)
+    yield
+    back = dot(da, s.up_one[...], NT)
+    s.grads[1, :, :] += dot(s.act_one[rows, :], da, TN)
+    yield
+    dz = (back * s.slope_one[rows, :]).astype(BF16)
+    branch = dot(dz, s.down_one[...])
+    s.grads[0, :, :] += dot(dz, s.out_low[rows, :], TN)
+    yield
+    dout = (dh + branch).astype(BF16)
+    s.ctx[rows, :] = dot(dout, s.w_out[...], NT).astype(BF16)
 
 
 def project_back(s, total, grads, target):
@@ -514,10 +533,10 @@
             start(1, step + 1, everyone)
 
         at_end = pl.when(final)
-        second_norm(s)
+        lockstep(second_norm(s, block) for block in blocks_of(s))
         start(2, step, everyone)
         feed_backward(s)
-        first_norm_backward(s)
+        lockstep(first_norm_backward(s, block) for block in [near_rows, *far_blocks(s)])
 
         @at_end
         def _():

time: 127 us -> 124 us (0.976)
  Pallas kernels: 126 us -> 123 us
    pallas_call x1, Pallas kernels: 121 us -> 118 us  [per_device(): pl.pallas_call(functools.partial(layer_kernel, parts, devices, per), out_...]
where the time goes in v7:
time: 124 us
  Pallas kernels  123 us (99%)
    pallas_call x1, Pallas kernels, per_device(): pl.pallas_call(functools.partial(layer_kernel, parts, devices, per), out_...  118 us
    pallas_call x1, Pallas kernels, per_device(): pl.pallas_call(tail_kernel, grid=(2,), out_shape=(moved, jax.ShapeDtypeSt...  5.19 us

profile of v7, /device:TPU:1, one launch (start us, length us, event | category | flops | bytes accessed | tf_op | source)
XLA Modules:
  0.0 124.1 jit_solution(1316365989077700874)
XLA Ops:
  0.6 118.1 %layer.1 = (bf16[12,128,768]{2,1,0:T(8,128)(2,1)}, bf16[12,128,768]{2,1,0:T(8,128)(2,1)}, bf16[2,16,8,896]{3,2,1,0:T(8,128)(2,1)}) custom-call(s32[12]{0:T(128)} %lengths.1, bf16[12,128,768]{2,1,0:T(8,128)(2,1)} %tokens.1, bf16[12,128,768]{2,1,0:T(8,128)(2,1)} %cotangent.1, bf16[768,768]{1,0:T(8,128)(2,1)} %refs_0_.1, bf16[768,768]{1,0:T(8,128)(2,1)} %refs_1_.1, ...), custom_call_target="tpu_custom_call" | custom-call | tf_op jit(solution)/shard_map/layer/pallas_call | solution.py:624
  118.8 5.2 %tail.1 = (bf16[12,128,768]{2,1,0:T(8,128)(2,1)}, f32[12,128,768]{2,1,0:T(8,128)}, f32[64,768]{1,0:T(8,128)}, f32[64,768]{1,0:T(8,128)}, f32[64,768]{1,0:T(8,128...) custom-call(bf16[12,128,768]{2,1,0:T(8,128)(2,1)} %get-tuple-element.23.output, ...), custom_call_target="tpu_custom_call" | custom-call | tf_op jit(solution)/shard_map/tail/pallas_call | solution.py:639

commit v8 on v7

--- a/solution.py
+++ b/solution.py
@@ -563,8 +563,9 @@
         if step == 0:
             two.fourth()
             one.fourth()
-    two.fifth()
-    one.fifth()
+        if step == per - 1:
+            two.fifth()
+            one.fifth()
     one.finish(4)
     two.finish(4)
 

time: 124 us -> 124 us (level)
  no operation moved by 1% of the time
where the time goes in v8:
time: 124 us
  Pallas kernels  123 us (99%)
    pallas_call x1, Pallas kernels, per_device(): pl.pallas_call(functools.partial(layer_kernel, parts, devices, per), out_...  118 us
    pallas_call x1, Pallas kernels, per_device(): pl.pallas_call(tail_kernel, grid=(2,), out_shape=(moved, jax.ShapeDtypeSt...  5.19 us

profile of v8, /device:TPU:1, one launch (start us, length us, event | category | flops | bytes accessed | tf_op | source)
XLA Modules:
  0.0 124.1 jit_solution(1316365989077700874)
XLA Ops:
  0.6 118.1 %layer.1 = (bf16[12,128,768]{2,1,0:T(8,128)(2,1)}, bf16[12,128,768]{2,1,0:T(8,128)(2,1)}, bf16[2,16,8,896]{3,2,1,0:T(8,128)(2,1)}) custom-call(s32[12]{0:T(128)} %lengths.1, bf16[12,128,768]{2,1,0:T(8,128)(2,1)} %tokens.1, bf16[12,128,768]{2,1,0:T(8,128)(2,1)} %cotangent.1, bf16[768,768]{1,0:T(8,128)(2,1)} %refs_0_.1, bf16[768,768]{1,0:T(8,128)(2,1)} %refs_1_.1, ...), custom_call_target="tpu_custom_call" | custom-call | tf_op jit(solution)/shard_map/layer/pallas_call | solution.py:625
  118.8 5.2 %tail.1 = (bf16[12,128,768]{2,1,0:T(8,128)(2,1)}, f32[12,128,768]{2,1,0:T(8,128)}, f32[64,768]{1,0:T(8,128)}, f32[64,768]{1,0:T(8,128)}, f32[64,768]{1,0:T(8,128...) custom-call(bf16[12,128,768]{2,1,0:T(8,128)(2,1)} %get-tuple-element.23.output, ...), custom_call_target="tpu_custom_call" | custom-call | tf_op jit(solution)/shard_map/tail/pallas_call | solution.py:640
